TPU v7x, 256 devices: a whole 4x4x8 slice. The times are simulated.
256 devices in a mesh: dp: 4 (over x), expert: 64 (over y, z, core).
Axes of the slice: x: 4, y: 4, z: 8, core: 2. Of those that a mesh axis runs over, the one named last changes fastest.
Arguments:
- tokens: bfloat16 [4096, 4096], P(('dp', 'expert')), may hold values from -6 to 6
- out_grad: bfloat16 [4096, 4096], P(('dp', 'expert')), may hold values from -6 to 6
- routes: int32 [4096, 8], P(('dp', 'expert')), may hold values from 0 to 63, all different within a row; in each aligned block of 16 rows (0 to 15, 16 to 31, ...) at most 4 rows name the same one
- router_weights: float32 [4096, 8], P(('dp', 'expert')), may hold values from 0.05 to 0.5
- w_gate: bfloat16 [64, 768, 4096], P('expert', 'dp'), may hold values from -0.09375 to 0.09375
- w_up: bfloat16 [64, 768, 4096], P('expert', 'dp'), may hold values from -0.09375 to 0.09375
- w_down: bfloat16 [64, 768, 4096], P('expert', 'dp'), may hold values from -0.21875 to 0.21875
Outputs:
- grad_tokens: bfloat16 [4096, 4096], P(('dp', 'expert'))
- grad_gate: bfloat16 [64, 768, 4096], P('expert', 'dp')
- grad_up: bfloat16 [64, 768, 4096], P('expert', 'dp')
- grad_down: bfloat16 [64, 768, 4096], P('expert', 'dp')
Inputs may be any that keep to these rules, and one draw needn't show every extreme that they name: `routes`: each token names 8 different experts; among the tokens of one device no expert is named more than 4 times, a bound that some block reaches.
All inputs are finite; a program needn't handle non-finite values.
Results may differ from a plain program's by a relative error of at most 0.015.
Values may be sent and summed in bfloat16 or wider, within the bound.
No kernel may reach another device: no remote copies, remote signals or barrier semaphores. Data moves between devices by JAX's collectives and lax.ppermute only.
A program may use at most 128 MiB of HBM per device.

v0:
```python
import functools

import jax
import jax.numpy as jnp
from jax import lax
from jax.experimental import pallas as pl
from jax.experimental.pallas import tpu as pltpu
from jax.sharding import Mesh
from jax.sharding import PartitionSpec as P

BF16 = jnp.bfloat16
F32 = jnp.float32
ALL = ("x", "y", "z", "c")


def shift(value, axis, by):
    size = lax.axis_size(axis)
    return lax.ppermute(value, axis, [(i, (i + by) % size) for i in range(size)])


def add(first, *others):
    total = first.astype(F32)
    for other in others:
        total = total + other.astype(F32)
    return total.astype(BF16)


def ring_ends(up, down, axis):
    return shift(up, axis, 1), shift(down, axis, -1)


def ring_ends4(opposite, axis):
    half = opposite.shape[0] // 2
    return ring_ends(opposite[:half], opposite[half:], axis)


def ring_middle4(near, back, ends):
    half = ends[0].shape[0]
    near = jnp.concatenate([add(near[:half], ends[0]), near[half:]], axis=0)
    back = jnp.concatenate([back[:half], add(back[half:], ends[1])], axis=0)
    return near, back


def ring_sum4(own, near, opposite, back, axis):
    near, back = ring_middle4(near, back, ring_ends4(opposite, axis))
    return add(own, *ring_ends(near, back, axis))


def ring_gather4(first, first_axis, second, second_axis, beside=()):
    near0, back0 = shift(first, first_axis, -1), shift(first, first_axis, 1)
    near1, back1 = shift(second, second_axis, -1), shift(second, second_axis, 1)
    near0, back0, near1, back1, beside = lax.optimization_barrier((near0, back0, near1, back1, beside))
    far = lambda near, back, axis, half: (shift(near[:half], axis, -1), shift(back[half:], axis, 1))
    far0 = far(near0, back0, first_axis, first.shape[0] // 2)
    far1 = far(near1, back1, second_axis, second.shape[0] // 2)
    return (first, near0, *far0, back0), (second, near1, *far1, back1), beside


def joined4(parts):
    own, near, first, second, back = parts
    return jnp.stack([own, near, jnp.concatenate([first, second], axis=0), back])


def ring_gather_z(left, right, axis):
    size, cut = lax.axis_size(axis), left.shape[1]
    own = jnp.concatenate([left, right], axis=1)
    up, down = [own], [own]
    for _ in range(size // 2 - 1):
        up.append(shift(up[-1], axis, -1))
        down.append(shift(down[-1], axis, 1))
    lefts = [b[:, :cut] for b in up] + [shift(up[-1][:, :cut], axis, -1)] + [b[:, :cut] for b in down[:0:-1]]
    rights = [b[:, cut:] for b in up] + [shift(down[-1][:, cut:], axis, 1)] + [b[:, cut:] for b in down[:0:-1]]
    return jnp.stack(lefts), jnp.stack(rights)


def expert_terms(ids, t, g, meta, wgu_ref, wd_ref, p_ref, dgu_ref, h_ref):
    rows, lanes = meta.shape
    hid = wd_ref.shape[0]
    lane = lax.rem(lax.broadcasted_iota(jnp.int32, (rows, lanes), 1), lanes // 2)
    values = meta.astype(F32)
    zero = jnp.float32(0)
    mine = jnp.sum(jnp.where(lane == ids[3], values, zero), axis=1, keepdims=True)
    other = jnp.sum(jnp.where(lane == ids[4], values, zero), axis=1, keepdims=True)
    column = lax.broadcasted_iota(jnp.int32, (rows, hid), 1)
    weight = jnp.where(column < hid // 2, mine, other)
    wide = (((1,), (1,)), ((), ()))
    gate_up = lax.dot_general(t, wgu_ref[...], wide, preferred_element_type=F32)
    back = lax.dot_general(g, wd_ref[...], wide, preferred_element_type=F32) * weight
    gate, upward = gate_up[:, :hid], gate_up[:, hid:]
    sigma = jax.nn.sigmoid(gate)
    active = gate * sigma
    hidden = (active * upward * weight).astype(BF16)
    d_gate = (back * upward * sigma * (1.0 + gate * (1.0 - sigma))).astype(BF16)
    d_up = (back * active).astype(BF16)
    both = jnp.concatenate([d_gate, d_up], axis=1)
    h_ref[...] = hidden.T.reshape(h_ref.shape)
    dgu_ref[...] = both.T.reshape(dgu_ref.shape)
    partial = jnp.dot(both, wgu_ref[...], preferred_element_type=F32)
    p_ref[...] = partial.astype(BF16).reshape(p_ref.shape)


def first_kernel(ids, t_ref, g_ref, m_ref, wgu_ref, wd_ref, p_ref, dgu_ref, h_ref):
    rows = t_ref.shape[1] * t_ref.shape[2] * t_ref.shape[5]
    flat = lambda ref: ref[...].reshape(rows, ref.shape[-1])
    expert_terms(ids, flat(t_ref), flat(g_ref), flat(m_ref), wgu_ref, wd_ref, p_ref, dgu_ref, h_ref)


def first_call(ids, rows, wgu, wd, lanes):
    nx, ny, nz, _, _, half, _ = rows.shape
    width = wgu.shape[1]
    hid = wd.shape[0]
    count = ny * nz * half
    at = lambda i, ids: lax.rem(ids[0] + i, nx)
    return pl.pallas_call(
        first_kernel,
        grid_spec=pltpu.PrefetchScalarGridSpec(
            num_scalar_prefetch=1,
            grid=(nx,),
            in_specs=[
                pl.BlockSpec((1, ny, nz, 1, 1, half, width), lambda i, ids: (at(i, ids), 0, 0, ids[2], 0, 0, 0)),
                pl.BlockSpec((1, ny, nz, 1, 1, half, width), lambda i, ids: (at(i, ids), 0, 0, ids[2], 1, 0, 0)),
                pl.BlockSpec(
                    (1, ny, nz, 1, 1, half, lanes), lambda i, ids: (at(i, ids), 0, 0, ids[2], 0, 0, width // lanes)
                ),
                pl.BlockSpec(wgu.shape, lambda i, ids: (0, 0), pipeline_mode=pl.Buffered(1)),
                pl.BlockSpec(wd.shape, lambda i, ids: (0, 0), pipeline_mode=pl.Buffered(1)),
            ],
            out_specs=[
                pl.BlockSpec((1, ny, nz, half, width), lambda i, ids: (i, 0, 0, 0, 0)),
                pl.BlockSpec((1, 2 * hid, count), lambda i, ids: (at(i, ids), 0, 0)),
                pl.BlockSpec((1, hid, count), lambda i, ids: (at(i, ids), 0, 0)),
            ],
        ),
        out_shape=[
            jax.ShapeDtypeStruct((nx, ny, nz, half, width), BF16),
            jax.ShapeDtypeStruct((nx, 2 * hid, count), BF16),
            jax.ShapeDtypeStruct((nx, hid, count), BF16),
        ],
        compiler_params=pltpu.CompilerParams(vmem_limit_bytes=56 << 20),
        name="tokens_first",
    )(ids, rows, rows, rows, wgu, wd)


def second_kernel(ids, *refs):
    t_parts, g_parts = refs[:5], refs[5:10]
    wgu_ref, wd_ref, p_ref, dgu_ref, h_ref, t_buf, g_buf, sems = refs[10:]
    step = pl.program_id(0)
    steps, half = t_buf.shape[1], t_buf.shape[1] // 2
    width = wgu_ref.shape[1]

    def copies(k):
        slot = k % 2
        if k == half:
            moves = [(t_parts[2], t_buf.at[slot, :half]), (t_parts[3], t_buf.at[slot, half:])]
        else:
            moves = [(t_parts[k if k < half else k + 1], t_buf.at[slot])]
        for y in range(steps):
            if y != half:
                source = g_parts[y if y < half else y + 1].at[k]
            elif k < half:
                source = g_parts[2].at[k]
            else:
                source = g_parts[3].at[k - half]
            moves.append((source, g_buf.at[slot, y]))
        return [pltpu.make_async_copy(a, b, sems.at[slot, n]) for n, (a, b) in enumerate(moves)]

    def run(k, method):
        for copy in copies(k):
            getattr(copy, method)()

    pl.when(step == 0)(lambda: run(0, "start"))
    for k in range(1, steps):
        pl.when(step == k - 1)(functools.partial(run, k, "start"))
    for k in range(steps):
        pl.when(step == k)(functools.partial(run, k, "wait"))
    slot = lax.rem(step, 2)
    rows = t_buf.shape[1] * t_buf.shape[2] * t_buf.shape[3]
    t = t_buf[slot, :, :, :, :width].reshape(rows, width)
    meta = t_buf[slot, :, :, :, width:].reshape(rows, -1)
    g = g_buf[slot].reshape(rows, width)
    expert_terms(ids, t, g, meta, wgu_ref, wd_ref, p_ref, dgu_ref, h_ref)


def second_call(ids, t_parts, g_parts, wgu, wd):
    ny, nz, half, wider = t_parts[0].shape
    nx, width = g_parts[0].shape[0], g_parts[0].shape[-1]
    hid = wd.shape[0]
    count = ny * nz * half
    hbm = pl.BlockSpec(memory_space=pl.ANY)
    return pl.pallas_call(
        second_kernel,
        grid_spec=pltpu.PrefetchScalarGridSpec(
            num_scalar_prefetch=1,
            grid=(nx,),
            in_specs=[hbm] * 10
            + [
                pl.BlockSpec(wgu.shape, lambda i, ids: (0, 0), pipeline_mode=pl.Buffered(1)),
                pl.BlockSpec(wd.shape, lambda i, ids: (0, 0), pipeline_mode=pl.Buffered(1)),
            ],
            out_specs=[
                pl.BlockSpec((ny, 1, nz, half, width), lambda i, ids: (0, i, 0, 0, 0)),
                pl.BlockSpec((1, 2 * hid, count), lambda i, ids: (i, 0, 0)),
                pl.BlockSpec((1, hid, count), lambda i, ids: (i, 0, 0)),
            ],
            scratch_shapes=[
                pltpu.VMEM((2, ny, nz, half, wider), BF16),
                pltpu.VMEM((2, ny, nz, half, width), BF16),
                pltpu.SemaphoreType.DMA((2, ny + 2)),
            ],
        ),
        out_shape=[
            jax.ShapeDtypeStruct((ny, nx, nz, half, width), BF16),
            jax.ShapeDtypeStruct((nx, 2 * hid, count), BF16),
            jax.ShapeDtypeStruct((nx, hid, count), BF16),
        ],
        compiler_params=pltpu.CompilerParams(vmem_limit_bytes=56 << 20),
        name="tokens_second",
    )(ids, *t_parts, *g_parts, wgu, wd)


def weight_kernel(ids, *refs):
    t_ref, g_ref = refs[:2]
    t_parts, g_parts = refs[2:7], refs[7:12]
    dgu0_ref, dgu1_ref, h0_ref, h1_ref, mine_ref, other_ref = refs[12:]
    nx, ny, nz, _, _, half, tile = t_ref.shape
    unit = h0_ref.shape[1] // 2
    flat = lambda a: a.reshape(-1, tile)

    def by_x(i):
        if i == nx // 2:
            return jnp.concatenate([flat(t_parts[2][...]), flat(t_parts[3][...])], axis=0)
        return flat(t_parts[i if i < nx // 2 else i + 1][...])

    def across(i):
        pieces = []
        for y in range(ny):
            if y != ny // 2:
                pieces.append(flat(g_parts[y if y < ny // 2 else y + 1][i]))
            else:
                pieces.append(flat(g_parts[2][i] if i < nx // 2 else g_parts[3][i - nx // 2]))
        return jnp.concatenate(pieces, axis=0)

    def outer(first, second, ref, right):
        total = None
        for i in range(nx):
            term = jnp.dot(first[i], flat(ref[i, :, :, 0, 0]), preferred_element_type=F32)
            total = term if total is None else total + term
        for i in range(nx):
            total = total + jnp.dot(second[i], right(i), preferred_element_type=F32)
        return total

    gu = outer(dgu0_ref, dgu1_ref, t_ref, by_x)
    down = outer(h0_ref, h1_ref, g_ref, across)
    mine_ref[0] = gu[:unit]
    mine_ref[1] = gu[2 * unit : 3 * unit]
    mine_ref[2] = down[:unit]
    other_ref[0] = gu[unit : 2 * unit].astype(BF16)
    other_ref[1] = gu[3 * unit :].astype(BF16)
    other_ref[2] = down[unit:].astype(BF16)


def weight_call(ids, rows, t_parts, g_parts, dgu0, dgu1, h0, h1):
    nx, ny, nz, _, _, half, _ = rows.shape
    width = g_parts[0].shape[-1]
    unit = h0.shape[1] // 2
    tile = 512
    whole = lambda a: pl.BlockSpec(a.shape, lambda j, ids: (0, 0, 0), pipeline_mode=pl.Buffered(1))
    part = lambda a: pl.BlockSpec((*a.shape[:3], tile), lambda j, ids: (0, 0, 0, j))
    return pl.pallas_call(
        weight_kernel,
        grid_spec=pltpu.PrefetchScalarGridSpec(
            num_scalar_prefetch=1,
            grid=(width // tile,),
            in_specs=[
                pl.BlockSpec((nx, ny, nz, 1, 1, half, tile), lambda j, ids: (0, 0, 0, ids[2], 0, 0, j)),
                pl.BlockSpec((nx, ny, nz, 1, 1, half, tile), lambda j, ids: (0, 0, 0, ids[2], 1, 0, j)),
                *(part(a) for a in t_parts),
                *(part(a) for a in g_parts),
                whole(dgu0),
                whole(dgu1),
                whole(h0),
                whole(h1),
            ],
            out_specs=[
                pl.BlockSpec((3, unit, tile), lambda j, ids: (0, 0, j)),
                pl.BlockSpec((3, unit, tile), lambda j, ids: (0, 0, j)),
            ],
        ),
        out_shape=[
            jax.ShapeDtypeStruct((3, unit, width), F32),
            jax.ShapeDtypeStruct((3, unit, width), BF16),
        ],
        compiler_params=pltpu.CompilerParams(vmem_limit_bytes=56 << 20),
        name="weights",
    )(ids, rows, rows, *t_parts, *g_parts, dgu0, dgu1, h0, h1)


def pick_weights(routes, router_weights, experts):
    hit = routes[:, :, None] == jnp.arange(experts, dtype=jnp.int32)[None, None, :]
    dense = jnp.sum(jnp.where(hit, router_weights[:, :, None], jnp.float32(0)), axis=1)
    high = lax.reduce_precision(dense, 8, 7)
    return jnp.concatenate([high, dense - high], axis=1).astype(BF16)


def on_device(tokens, out_grad, routes, router_weights, w_gate, w_up, w_down):
    nx, ny, nz, nc = (lax.axis_size(a) for a in ALL)
    ix, iy, iz, ic = (lax.axis_index(a) for a in ALL)
    per, width = tokens.shape
    half = per // 2
    experts = ny * nz * nc
    expert = (iy * nz + iz) * nc + ic
    ids = jnp.stack([ix, iy, ic, expert, expert + 1 - 2 * ic]).astype(jnp.int32)

    meta = pick_weights(routes, router_weights, experts)
    lanes = meta.shape[1]
    wider = jnp.concatenate([tokens, meta], axis=1)
    grads0 = jnp.concatenate([out_grad[:half], jnp.zeros((half, lanes), BF16)], axis=1)
    rows = lax.all_gather(jnp.concatenate([wider[:half], grads0], axis=0), ALL, axis=0, tiled=True)
    rows = rows.reshape(nx, ny, nz, nc, 2, half, width + lanes)

    t_z, g_z = ring_gather_z(wider[half:], out_grad[half:], "z")
    t_y, g_x, _ = ring_gather4(t_z, "y", g_z, "x")
    t_y, g_x = lax.optimization_barrier((joined4(t_y), joined4(g_x)))

    w_gate, w_up, w_down, _ = lax.optimization_barrier((w_gate, w_up, w_down, t_y))
    packed = jnp.concatenate([w_gate, w_up, w_down], axis=0)
    swapped = shift(packed, "c", 1)
    wgu = jnp.concatenate([w_gate[0], swapped[0], w_up[0], swapped[1]], axis=0)
    wd = jnp.concatenate([w_down[0], swapped[2]], axis=0)
    t_parts, g_parts, (wgu, wd) = ring_gather4(t_y, "x", g_x, "y", (wgu, wd))

    p1, dgu1, h1 = second_call(ids, t_parts, g_parts, wgu, wd)
    ends1 = ring_ends4(p1[2], "y")
    rows, dgu1 = lax.optimization_barrier((rows, dgu1))
    p0, dgu0, h0 = first_call(ids, rows, wgu, wd, lanes)
    ends1, p0, dgu0, h0 = lax.optimization_barrier((ends1, p0, dgu0, h0))
    ends0 = ring_ends4(p0[2], "x")
    near1, back1 = ring_middle4(p1[1], p1[3], ends1)
    last1 = ring_ends(near1, back1, "y")
    near0, back0 = ring_middle4(p0[1], p0[3], ends0)
    near0, back0, dgu0 = lax.optimization_barrier((near0, back0, dgu0))
    last0 = ring_ends(near0, back0, "x")
    mine, other = weight_call(ids, rows, t_parts, g_parts, dgu0, dgu1, h0, h1)
    last1, mine, other = lax.optimization_barrier((last1, mine, other))
    q1 = add(p1[0], *last1)
    r1 = ring_sum4(q1[0], q1[1], q1[2], q1[3], "x")
    r1 = lax.dynamic_slice_in_dim(jnp.concatenate([r1, r1], axis=0), nz - iz, nz, axis=0)
    q0 = add(p0[0], *last0)
    pick = lambda k: lax.dynamic_index_in_dim(q0, lax.rem(iy + k, ny), 0, keepdims=False)
    r0 = ring_sum4(pick(0), pick(1), pick(2), pick(3), "y")
    scatter = lambda r: lax.psum_scatter(r.reshape(nz * half, width), "z", scatter_dimension=0, tiled=True)
    grad_tokens = jnp.concatenate([scatter(r0), scatter(r1)], axis=0)

    grads = (mine + shift(other, "c", 1).astype(F32)).astype(BF16)
    return grad_tokens, grads[0:1], grads[1:2], grads[2:3]


def solution(mesh):
    fine = Mesh(mesh.devices.reshape(4, 4, 8, 2), ALL)
    row = P(ALL, None)
    weight = P(("y", "z", "c"), "x", None)
    return jax.shard_map(
        on_device,
        mesh=fine,
        in_specs=(row, row, row, row, weight, weight, weight),
        out_specs=(row, weight, weight, weight),
        check_vma=False,
    )
```

profile of v0, /device:TPU:8, one launch (start us, length us, event | category | flops | bytes accessed | tf_op | source)
XLA Modules:
  0.0 508.2 jit_solution(8574142743664673991)
XLA Ops:
  11.5 5.9 %collective-permute-start = (bf16[8,8320]{1,0:T(8,128)(2,1)S(1)}, bf16[8,8320]{1,0:T(8,128)(2,1)S(1)}, u32[]{:S(2)}, u32[]{:S(2)}) collective-permute-start(bf16[8,8320]{1,0:T(8,128)(2,1)S(1)} %pad_maximum_fusion.13), channel_id=1, source_target_pairs={{0,14},{2,0},{4,2},{6,4},{8,6},{10,8},{12,10},{14,12},{1,15},{3,1}... | collective-permute-start | bytes 399368 | tf_op jit(solution)/shard_map/ppermute | solution.py:18
  18.3 1.9 collective-permute-done
  20.3 3.7 collective-permute-start.1
  24.0 2.5 collective-permute-done.1
  26.5 3.7 collective-permute-start.2
  30.2 2.5 collective-permute-done.2
  32.7 3.7 collective-permute-start.3
  36.5 5.5 %collective-permute-done.9 = bf16[8,4096]{1,0:T(8,128)(2,1)S(1)} collective-permute-done((bf16[8,4096]{1,0:T(8,128)(2,1)S(1)}, bf16[8,4096]{1,0:T(8,128)(2,1)S(1)}, u32[]{:S(2)}, u32[]{:S(2)}) %collective-permute-start.9) | collective-permute-done | bytes 65568 | tf_op jit(solution)/shard_map/ppermute | solution.py:18
  42.7 1.5 collective-permute-start.8
  44.2 3.0 collective-permute-start.10
  47.2 6.8 %collective-permute-done.10 = bf16[8,8,4096]{2,1,0:T(8,128)(2,1)S(1)} collective-permute-done((bf16[8,8,4096]{2,1,0:T(8,128)(2,1)S(1)}, bf16[8,8,4096]{2,1,0:T(8,128)(2,1)S(1)}, u32[]{:S(2)}, u32[]{:S(2)}) %collective-permute-start.10) | collective-permute-done | bytes 524320 | tf_op jit(solution)/shard_map/ppermute | solution.py:18
  54.0 5.6 %collective-permute-done.11 = bf16[8,8,4096]{2,1,0:T(8,128)(2,1)S(1)} collective-permute-done((bf16[8,8,4096]{2,1,0:T(8,128)(2,1)S(1)}, bf16[8,8,4096]{2,1,0:T(8,128)(2,1)S(1)}, u32[]{:S(2)}, u32[]{:S(2)}) %collective-permute-start.11) | collective-permute-done | bytes 524320 | tf_op jit(solution)/shard_map/ppermute | solution.py:18
  59.8 3.3 collective-permute-start.14
  63.1 1.8 collective-permute-start.13
  65.7 1.7 collective-permute-done.15
  67.4 2.7 collective-permute-done.14
  71.0 1.9 collective-permute-done.12
  75.9 2.1 collective-permute-start.16
  78.0 2.5 collective-permute-start.18
  80.5 3.3 collective-permute-done.20
  84.3 1.9 pad_maximum_fusion.2.refs_11_.wd_ref
  86.1 11.1 %pad_maximum_fusion.refs_10_.wgu_ref = bf16[768,4096]{1,0:T(8,128)(2,1)} fusion(bf16[192,4096]{1,0:T(8,128)(2,1)S(1)} %get-tuple-element.94, bf16[192,4096]{1,0:T(8,128)(2,1)S(1)} %bitcast.164, bf16[192,4096]{1,0:T(8,128)(2,1)S(1)} %get-tuple-element.95, bf16[192,4096]{1,0:T(8,128)(2,1)S(1)} %bitcast.165), kind=kLoop, calls=%fused_computation.1 | loop fusion | flops 25165824 | bytes 12582912 | tf_op jit(solution)/shard_map/concatenate | solution.py:328
  97.3 49.7 %collective-permute-done.18.refs_6_.refs_8_ = bf16[4,8,8,4096]{3,2,1,0:T(8,128)(2,1)S(1)} collective-permute-done((bf16[4,8,8,4096]{3,2,1,0:T(8,128)(2,1)S(1)}, bf16[4,8,8,4096]{3,2,1,0:T(8,128)(2,1)S(1)}, u32[]{:S(2)}, u32[]{:S(2)}) %collective-permute-start.18) | collective-permute-done | bytes 2097184 | tf_op jit(solution)/shard_map/ppermute | solution.py:18
  147.0 8.3 %collective-permute-done.19.refs_9_.refs_11_ = bf16[4,8,8,4096]{3,2,1,0:T(8,128)(2,1)S(1)} collective-permute-done((bf16[4,8,8,4096]{3,2,1,0:T(8,128)(2,1)S(1)}, bf16[4,8,8,4096]{3,2,1,0:T(8,128)(2,1)S(1)}, u32[]{:S(2)}, u32[]{:S(2)}) %collective-permute-start.19) | collective-permute-done | bytes 2097184 | tf_op jit(solution)/shard_map/ppermute | solution.py:18
  155.3 1.1 slice.277
  156.4 3.4 collective-permute-start.21
  162.0 3.5 collective-permute-start.23
  165.5 1.1 slice.280
  167.4 28.5 %collective-permute-done.23.refs_7_.refs_9_ = bf16[2,8,8,4096]{3,2,1,0:T(8,128)(2,1)S(1)} collective-permute-done((bf16[2,8,8,4096]{3,2,1,0:T(8,128)(2,1)}, bf16[2,8,8,4096]{3,2,1,0:T(8,128)(2,1)S(1)}, u32[]{:S(2)}, u32[]{:S(2)}) %collective-permute-start.23) | collective-permute-done | bytes 1048608 | tf_op jit(solution)/shard_map/ppermute | solution.py:18
  195.9 3.5 collective-permute-done.24.refs_8_.refs_10_
  201.4 32.4 %tokens_second.1 = (bf16[4,4,8,8,4096]{4,3,2,1,0:T(8,128)(2,1)}, bf16[4,768,256]{2,1,0:T(8,128)(2,1)}, bf16[4,384,256]{2,1,0:T(8,128)(2,1)}) custom-call(s32[5]{0:T(128)} %stack.107.ids, bf16[4,8,8,4224]{3,2,1,0:T(8,128)(2,1)} %copy-done, bf16[4,8,8,4224]{3,2,1,0:T(8,128)(2,1)} %copy-done.2, bf16[2,8,8,4224]{3,2,1,0:T(8,128)(2,1)} %copy-done.10, ...), custom_call_target="tpu_custom_call" | custom-call | tf_op jit(solution)/shard_map/tokens_second/pallas_call | solution.py:190
  233.8 3.9 slice_bitcast_fusion.3
  238.2 2.1 collective-permute-start.26
  240.3 31.0 %tokens_first.1 = (bf16[4,4,8,8,4096]{4,3,2,1,0:T(8,128)(2,1)}, bf16[4,768,256]{2,1,0:T(8,128)(2,1)}, bf16[4,384,256]{2,1,0:T(8,128)(2,1)}) custom-call(s32[5]{0:T(128)} %stack.107.ids, bf16[4,4,8,2,2,8,4224]{6,5,4,3,2,1,0:T(8,128)(2,1)} %bitcast.159, bf16[4,4,8,2,2,8,4224]{6,5,4,3,2,1,0:T(8,128)(2,1)} %bitcast.160, ...), custom_call_target="tpu_custom_call" | custom-call | tf_op jit(solution)/shard_map/tokens_first/pallas_call | solution.py:114
  271.3 2.5 slice_bitcast_fusion.6
  273.8 3.1 collective-permute-start.28
  277.1 2.6 fusion.4
  280.3 3.1 collective-permute-start.36
  283.5 14.1 %collective-permute-done.28 = bf16[2,8,8,4096]{3,2,1,0:T(8,128)(2,1)S(1)} collective-permute-done((bf16[2,8,8,4096]{3,2,1,0:T(8,128)(2,1)S(1)}, bf16[2,8,8,4096]{3,2,1,0:T(8,128)(2,1)S(1)}, u32[]{:S(2)}, u32[]{:S(2)}) %collective-permute-start.28) | collective-permute-done | bytes 1048608 | tf_op jit(solution)/shard_map/ppermute | solution.py:18
  297.5 3.4 collective-permute-done.27
  300.9 2.3 fusion.6
  303.2 2.4 pad_maximum_fusion.5
  305.6 27.2 %weights.1 = (f32[3,192,4096]{2,1,0:T(8,128)}, bf16[3,192,4096]{2,1,0:T(8,128)(2,1)}) custom-call(s32[5]{0:T(128)} %stack.107.ids, bf16[4,4,8,2,2,8,4224]{6,5,4,3,2,1,0:T(8,128)(2,1)} %bitcast.162, bf16[4,4,8,2,2,8,4224]{6,5,4,3,2,1,0:T(8,128)(2,1)} %bitcast.163, bf16[4,8,8,4224]{3,2,1,0:T(8,128)(2,1)} %copy-done, bf16[4,8,8,4224]{3,2,1,0:T(8,128)(2,1)} %copy-done.2, ...), custom_call_target="tpu_custom_call" | custom-call | tf_op jit(solution)/shard_map/weights/pallas_call | solution.py:269
  332.8 1.3 copy-done.13
  334.2 3.9 fusion.1
  339.0 3.2 collective-permute-start.39
  342.3 2.0 collective-permute-start.29
  344.3 5.4 %collective-permute-done.37 = bf16[4,8,4096]{2,1,0:T(8,128)(2,1)S(1)} collective-permute-done((bf16[4,8,4096]{2,1,0:T(8,128)(2,1)}, bf16[4,8,4096]{2,1,0:T(8,128)(2,1)S(1)}, u32[]{:S(2)}, u32[]{:S(2)}) %collective-permute-start.37) | collective-permute-done | bytes 262176 | tf_op jit(solution)/shard_map/ppermute | solution.py:18
  349.9 3.1 collective-permute-start.40
  353.4 40.7 %collective-permute-done.30 = bf16[4,8,8,4096]{3,2,1,0:T(8,128)(2,1)} collective-permute-done((bf16[4,8,8,4096]{3,2,1,0:T(8,128)(2,1)}, bf16[4,8,8,4096]{3,2,1,0:T(8,128)(2,1)}, u32[]{:S(2)}, u32[]{:S(2)}) %collective-permute-start.30) | collective-permute-done | bytes 2097184 | tf_op jit(solution)/shard_map/ppermute | solution.py:18
  394.7 3.9 fusion.3
  398.8 1.3 collective-permute-start.31
  400.1 1.8 collective-permute-start.33
  401.9 1.2 fusion.9
  403.1 4.0 collective-permute-done.31
  407.1 2.0 collective-permute-done.33
  410.0 2.7 collective-permute-start.34
  414.6 5.2 %collective-permute-done.34 = bf16[8,8,4096]{2,1,0:T(8,128)(2,1)S(1)} collective-permute-done((bf16[8,8,4096]{2,1,0:T(8,128)(2,1)}, bf16[8,8,4096]{2,1,0:T(8,128)(2,1)S(1)}, u32[]{:S(2)}, u32[]{:S(2)}) %collective-permute-start.34) | collective-permute-done | bytes 524320 | tf_op jit(solution)/shard_map/ppermute | solution.py:18
  419.9 4.7 collective-permute-done.32
  425.6 25.9 %reduce-scatter.5.cloned.1.call-done = bf16[8,4096]{1,0:T(8,128)(2,1)} async-done(((bf16[64,4096]{1,0:T(8,128)(2,1)}), bf16[8,4096]{1,0:T(8,128)(2,1)}) %reduce-scatter.5.cloned.1.call-update) | async-done | bytes 65552 | tf_op jit(solution)/shard_map/reduce_scatter | solution.py:351
  451.6 39.2 %reduce-scatter.3.cloned.1.call-done = bf16[8,4096]{1,0:T(8,128)(2,1)} async-done(((bf16[64,4096]{1,0:T(8,128)(2,1)}), bf16[8,4096]{1,0:T(8,128)(2,1)}) %reduce-scatter.3.cloned.1.call-update) | async-done | bytes 65552 | tf_op jit(solution)/shard_map/reduce_scatter | solution.py:351
  490.8 1.5 pad_maximum_fusion.14
  492.3 6.6 %add_convert_fusion = bf16[3,192,4096]{2,1,0:T(8,128)(2,1)S(1)} fusion(f32[3,192,4096]{2,1,0:T(8,128)} %get-tuple-element.76, bf16[3,192,4096]{2,1,0:T(8,128)(2,1)} %collective-permute-done.41), kind=kLoop, calls=%fused_computation | loop fusion | flops 7077888 | bytes 18874368 | tf_op jit(solution)/shard_map/convert_element_type | solution.py:354
  498.9 2.3 fusion.32
  (127 shorter events, 23.6 us)
Async XLA Ops:
  7.2 233.1 %all-gather.2.cloned.1.call-start = ((), (), s32[]{:S(2)}) async-start(), calls=%async_computation.2 | async-start | bytes 34738176 | tf_op jit(solution)/shard_map/all_gather | solution.py:318
  11.5 440.1 %reduce-scatter.5.cloned.1.call-start = ((), (), s32[]{:S(2)}) async-start(), calls=%async_computation.4 | async-start | bytes 589824 | tf_op jit(solution)/shard_map/reduce_scatter | solution.py:351
  11.5 8.7 %collective-permute-start = (bf16[8,8320]{1,0:T(8,128)(2,1)S(1)}, bf16[8,8320]{1,0:T(8,128)(2,1)S(1)}, u32[]{:S(2)}, u32[]{:S(2)}) collective-permute-start(bf16[8,8320]{1,0:T(8,128)(2,1)S(1)} %pad_maximum_fusion.13), channel_id=1, source_target_pairs={{0,14},{2,0},{4,2},{6,4},{8,6},{10,8},{12,10},{14,12},{1,15},{3,1}... | collective-permute-start | bytes 399368 | tf_op jit(solution)/shard_map/ppermute | solution.py:18
  17.5 6.5 %collective-permute-start.4 = (bf16[8,8320]{1,0:T(8,128)(2,1)S(1)}, bf16[8,8320]{1,0:T(8,128)(2,1)S(1)}, u32[]{:S(2)}, u32[]{:S(2)}) collective-permute-start(bf16[8,8320]{1,0:T(8,128)(2,1)S(1)} %pad_maximum_fusion.13), channel_id=1, source_target_pairs={{0,2},{2,4},{4,6},{6,8},{8,10},{10,12},{12,14},{14,0},{1,3},{3,5},... | collective-permute-start | bytes 399368 | tf_op jit(solution)/shard_map/ppermute | solution.py:18
  20.3 6.2 %collective-permute-start.1 = (bf16[8,8320]{1,0:T(8,128)(2,1)S(1)}, bf16[8,8320]{1,0:T(8,128)(2,1)S(1)}, u32[]{:S(2)}, u32[]{:S(2)}) collective-permute-start(bf16[8,8320]{1,0:T(8,128)(2,1)S(1)} %collective-permute-done), channel_id=1, source_target_pairs={{0,14},{2,0},{4,2},{6,4},{8,6},{10,8},{12,10},{14,12},{1,15},{3,1}... | collective-permute-start | bytes 399368 | tf_op jit(solution)/shard_map/ppermute | solution.py:18
  23.9 6.2 %collective-permute-start.5 = (bf16[8,8320]{1,0:T(8,128)(2,1)S(1)}, bf16[8,8320]{1,0:T(8,128)(2,1)S(1)}, u32[]{:S(2)}, u32[]{:S(2)}) collective-permute-start(bf16[8,8320]{1,0:T(8,128)(2,1)S(1)} %collective-permute-done.4), channel_id=1, source_target_pairs={{0,2},{2,4},{4,6},{6,8},{8,10},{10,12},{12,14},{14,0},{1,3},{3,5},... | collective-permute-start | bytes 399368 | tf_op jit(solution)/shard_map/ppermute | solution.py:18
  26.5 6.2 %collective-permute-start.2 = (bf16[8,8320]{1,0:T(8,128)(2,1)S(1)}, bf16[8,8320]{1,0:T(8,128)(2,1)S(1)}, u32[]{:S(2)}, u32[]{:S(2)}) collective-permute-start(bf16[8,8320]{1,0:T(8,128)(2,1)S(1)} %collective-permute-done.1), channel_id=1, source_target_pairs={{0,14},{2,0},{4,2},{6,4},{8,6},{10,8},{12,10},{14,12},{1,15},{3,1}... | collective-permute-start | bytes 399368 | tf_op jit(solution)/shard_map/ppermute | solution.py:18
  30.1 6.3 %collective-permute-start.6 = (bf16[8,8320]{1,0:T(8,128)(2,1)S(1)}, bf16[8,8320]{1,0:T(8,128)(2,1)S(1)}, u32[]{:S(2)}, u32[]{:S(2)}) collective-permute-start(bf16[8,8320]{1,0:T(8,128)(2,1)S(1)} %collective-permute-done.5), channel_id=1, source_target_pairs={{0,2},{2,4},{4,6},{6,8},{8,10},{10,12},{12,14},{14,0},{1,3},{3,5},... | collective-permute-start | bytes 399368 | tf_op jit(solution)/shard_map/ppermute | solution.py:18
  32.7 9.3 %collective-permute-start.3 = (bf16[8,4224]{1,0:T(8,128)(2,1)S(1)}, bf16[8,4224]{1,0:T(8,128)(2,1)S(1)}, u32[]{:S(2)}, u32[]{:S(2)}) collective-permute-start(bf16[8,4224]{1,0:T(8,128)(2,1)S(1)} %slice.332), channel_id=1, source_target_pairs={{0,14},{2,0},{4,2},{6,4},{8,6},{10,8},{12,10},{14,12},{1,15},{3,1}... | collective-permute-start | bytes 202760 | tf_op jit(solution)/shard_map/ppermute | solution.py:18
  36.4 5.6 %collective-permute-start.9 = (bf16[8,4096]{1,0:T(8,128)(2,1)S(1)}, bf16[8,4096]{1,0:T(8,128)(2,1)S(1)}, u32[]{:S(2)}, u32[]{:S(2)}) collective-permute-start(bf16[8,4096]{1,0:T(8,128)(2,1)S(1)} %slice.339), channel_id=1, source_target_pairs={{0,2},{2,4},{4,6},{6,8},{8,10},{10,12},{12,14},{14,0},{1,3},{3,5},... | collective-permute-start | bytes 196616 | tf_op jit(solution)/shard_map/ppermute | solution.py:18
  42.1 17.6 %collective-permute-start.7 = (bf16[8,8,4224]{2,1,0:T(8,128)(2,1)S(1)}, bf16[8,8,4224]{2,1,0:T(8,128)(2,1)S(1)}, u32[]{:S(2)}, u32[]{:S(2)}) collective-permute-start(bf16[8,8,4224]{2,1,0:T(8,128)(2,1)S(1)} %fusion.21), channel_id=1, source_target_pairs={{0,48},{16,0},{32,16},{48,32},{1,49},{17,1},{33,17},{49,33},{2,50}... | collective-permute-start | bytes 1622024 | tf_op jit(solution)/shard_map/ppermute | solution.py:18
  42.7 16.9 %collective-permute-start.8 = (bf16[8,8,4224]{2,1,0:T(8,128)(2,1)S(1)}, bf16[8,8,4224]{2,1,0:T(8,128)(2,1)S(1)}, u32[]{:S(2)}, u32[]{:S(2)}) collective-permute-start(bf16[8,8,4224]{2,1,0:T(8,128)(2,1)S(1)} %fusion.21), channel_id=1, source_target_pairs={{0,16},{16,32},{32,48},{48,0},{1,17},{17,33},{33,49},{49,1},{2,18}... | collective-permute-start | bytes 1622024 | tf_op jit(solution)/shard_map/ppermute | solution.py:18
  44.2 9.8 %collective-permute-start.10 = (bf16[8,8,4096]{2,1,0:T(8,128)(2,1)S(1)}, bf16[8,8,4096]{2,1,0:T(8,128)(2,1)S(1)}, u32[]{:S(2)}, u32[]{:S(2)}) collective-permute-start(bf16[8,8,4096]{2,1,0:T(8,128)(2,1)S(1)} %fusion.26), channel_id=1, source_target_pairs={{0,192},{64,0},{128,64},{192,128},{1,193},{65,1},{129,65},{193,129... | collective-permute-start | bytes 1572872 | tf_op jit(solution)/shard_map/ppermute | solution.py:18
  47.2 12.4 %collective-permute-start.11 = (bf16[8,8,4096]{2,1,0:T(8,128)(2,1)S(1)}, bf16[8,8,4096]{2,1,0:T(8,128)(2,1)S(1)}, u32[]{:S(2)}, u32[]{:S(2)}) collective-permute-start(bf16[8,8,4096]{2,1,0:T(8,128)(2,1)S(1)} %fusion.26), channel_id=1, source_target_pairs={{0,64},{64,128},{128,192},{192,0},{1,65},{65,129},{129,193},{193,1... | collective-permute-start | bytes 1572872 | tf_op jit(solution)/shard_map/ppermute | solution.py:18
  59.7 7.7 %collective-permute-start.15 = (bf16[4,8,4096]{2,1,0:T(8,128)(2,1)S(1)}, bf16[4,8,4096]{2,1,0:T(8,128)(2,1)S(1)}, u32[]{:S(2)}, u32[]{:S(2)}) collective-permute-start(bf16[4,8,4096]{2,1,0:T(8,128)(2,1)S(1)} %slice.273), channel_id=1, source_target_pairs={{0,64},{64,128},{128,192},{192,0},{1,65},{65,129},{129,193},{193,1... | collective-permute-start | bytes 786440 | tf_op jit(solution)/shard_map/ppermute | solution.py:18
  59.8 10.3 %collective-permute-start.14 = (bf16[4,8,4096]{2,1,0:T(8,128)(2,1)S(1)}, bf16[4,8,4096]{2,1,0:T(8,128)(2,1)S(1)}, u32[]{:S(2)}, u32[]{:S(2)}) collective-permute-start(bf16[4,8,4096]{2,1,0:T(8,128)(2,1)S(1)} %slice.272), channel_id=1, source_target_pairs={{0,192},{64,0},{128,64},{192,128},{1,193},{65,1},{129,65},{193,129... | collective-permute-start | bytes 786440 | tf_op jit(solution)/shard_map/ppermute | solution.py:18
  63.1 7.8 %collective-permute-start.13 = (bf16[4,8,4224]{2,1,0:T(8,128)(2,1)S(1)}, bf16[4,8,4224]{2,1,0:T(8,128)(2,1)S(1)}, u32[]{:S(2)}, u32[]{:S(2)}) collective-permute-start(bf16[4,8,4224]{2,1,0:T(8,128)(2,1)S(1)} %slice.271), channel_id=1, source_target_pairs={{0,16},{16,32},{32,48},{48,0},{1,17},{17,33},{33,49},{49,1},{2,18}... | collective-permute-start | bytes 811016 | tf_op jit(solution)/shard_map/ppermute | solution.py:18
  64.9 7.9 %collective-permute-start.12 = (bf16[4,8,4224]{2,1,0:T(8,128)(2,1)S(1)}, bf16[4,8,4224]{2,1,0:T(8,128)(2,1)S(1)}, u32[]{:S(2)}, u32[]{:S(2)}) collective-permute-start(bf16[4,8,4224]{2,1,0:T(8,128)(2,1)S(1)} %slice.270), channel_id=1, source_target_pairs={{0,48},{16,0},{32,16},{48,32},{1,49},{17,1},{33,17},{49,33},{2,50}... | collective-permute-start | bytes 811016 | tf_op jit(solution)/shard_map/ppermute | solution.py:18
  70.4 10.0 %copy-start.1 = (bf16[4,8,8,4096]{3,2,1,0:T(8,128)(2,1)}, bf16[4,8,8,4096]{3,2,1,0:T(8,128)(2,1)S(1)}, u32[]{:S(2)}) copy-start(bf16[4,8,8,4096]{3,2,1,0:T(8,128)(2,1)S(1)} %pad_maximum_fusion.4.refs_5_.refs_7_) | copy-start | bytes 6291460
  72.9 1.4 copy-start.9
  72.9 1.9 copy-start.7
  72.9 2.3 copy-start.8
  75.3 2.8 copy-start
  75.8 8.0 %collective-permute-start.20 = (bf16[3,192,4096]{2,1,0:T(8,128)(2,1)S(1)}, bf16[3,192,4096]{2,1,0:T(8,128)(2,1)S(1)}, u32[]{:S(2)}, u32[]{:S(2)}) collective-permute-start(bf16[3,192,4096]{2,1,0:T(8,128)(2,1)S(1)} %pad_maximum_fusion.1), channel_id=1, source_target_pairs={{0,1},{1,0},{2,3},{3,2},{4,5},{5,4},{6,7},{7,6},{8,9},{9,8},{10,11... | collective-permute-start | bytes 14155784 | tf_op jit(solution)/shard_map/ppermute | solution.py:18
  75.9 79.3 %collective-permute-start.16 = (bf16[4,8,8,4224]{3,2,1,0:T(8,128)(2,1)S(1)}, bf16[4,8,8,4224]{3,2,1,0:T(8,128)(2,1)S(1)}, u32[]{:S(2)}, u32[]{:S(2)}) collective-permute-start(bf16[4,8,8,4224]{3,2,1,0:T(8,128)(2,1)S(1)} %pad_maximum_fusion.3.refs_0_.refs_2_), channel_id=1, source_target_pairs={{0,192},{64,0},{128,64},{192,128},{1,193},{65,1},{129,65},{193,129... | collective-permute-start | bytes 6488072 | tf_op jit(solution)/shard_map/ppermute | solution.py:18
  78.0 77.2 %collective-permute-start.17 = (bf16[4,8,8,4224]{3,2,1,0:T(8,128)(2,1)S(1)}, bf16[4,8,8,4224]{3,2,1,0:T(8,128)(2,1)S(1)}, u32[]{:S(2)}, u32[]{:S(2)}) collective-permute-start(bf16[4,8,8,4224]{3,2,1,0:T(8,128)(2,1)S(1)} %pad_maximum_fusion.3.refs_0_.refs_2_), channel_id=1, source_target_pairs={{0,64},{64,128},{128,192},{192,0},{1,65},{65,129},{129,193},{193,1... | collective-permute-start | bytes 6488072 | tf_op jit(solution)/shard_map/ppermute | solution.py:18
  78.0 69.0 %collective-permute-start.18 = (bf16[4,8,8,4096]{3,2,1,0:T(8,128)(2,1)S(1)}, bf16[4,8,8,4096]{3,2,1,0:T(8,128)(2,1)S(1)}, u32[]{:S(2)}, u32[]{:S(2)}) collective-permute-start(bf16[4,8,8,4096]{3,2,1,0:T(8,128)(2,1)S(1)} %pad_maximum_fusion.4.refs_5_.refs_7_), channel_id=1, source_target_pairs={{0,48},{16,0},{32,16},{48,32},{1,49},{17,1},{33,17},{49,33},{2,50}... | collective-permute-start | bytes 6291464 | tf_op jit(solution)/shard_map/ppermute | solution.py:18
  80.5 74.8 %collective-permute-start.19 = (bf16[4,8,8,4096]{3,2,1,0:T(8,128)(2,1)S(1)}, bf16[4,8,8,4096]{3,2,1,0:T(8,128)(2,1)S(1)}, u32[]{:S(2)}, u32[]{:S(2)}) collective-permute-start(bf16[4,8,8,4096]{3,2,1,0:T(8,128)(2,1)S(1)} %pad_maximum_fusion.4.refs_5_.refs_7_), channel_id=1, source_target_pairs={{0,16},{16,32},{32,48},{48,0},{1,17},{17,33},{33,49},{49,1},{2,18}... | collective-permute-start | bytes 6291464 | tf_op jit(solution)/shard_map/ppermute | solution.py:18
  147.0 13.9 %copy-start.4 = (bf16[4,8,8,4096]{3,2,1,0:T(8,128)(2,1)}, bf16[4,8,8,4096]{3,2,1,0:T(8,128)(2,1)S(1)}, u32[]{:S(2)}) copy-start(bf16[4,8,8,4096]{3,2,1,0:T(8,128)(2,1)S(1)} %collective-permute-done.18.refs_6_.refs_8_) | copy-start | bytes 6291460
  155.3 10.2 %copy-start.5 = (bf16[4,8,8,4096]{3,2,1,0:T(8,128)(2,1)}, bf16[4,8,8,4096]{3,2,1,0:T(8,128)(2,1)S(1)}, u32[]{:S(2)}) copy-start(bf16[4,8,8,4096]{3,2,1,0:T(8,128)(2,1)S(1)} %collective-permute-done.19.refs_9_.refs_11_) | copy-start | bytes 6291460
  155.3 5.7 %copy-start.2 = (bf16[4,8,8,4224]{3,2,1,0:T(8,128)(2,1)}, bf16[4,8,8,4224]{3,2,1,0:T(8,128)(2,1)S(1)}, u32[]{:S(2)}) copy-start(bf16[4,8,8,4224]{3,2,1,0:T(8,128)(2,1)S(1)} %collective-permute-done.16.refs_1_.refs_3_) | copy-start | bytes 6488068
  155.3 5.7 %copy-start.3 = (bf16[4,8,8,4224]{3,2,1,0:T(8,128)(2,1)}, bf16[4,8,8,4224]{3,2,1,0:T(8,128)(2,1)S(1)}, u32[]{:S(2)}) copy-start(bf16[4,8,8,4224]{3,2,1,0:T(8,128)(2,1)S(1)} %collective-permute-done.17.refs_4_.refs_6_) | copy-start | bytes 6488068
  156.4 43.0 %collective-permute-start.21 = (bf16[2,8,8,4224]{3,2,1,0:T(8,128)(2,1)}, bf16[2,8,8,4224]{3,2,1,0:T(8,128)(2,1)S(1)}, u32[]{:S(2)}, u32[]{:S(2)}) collective-permute-start(bf16[2,8,8,4224]{3,2,1,0:T(8,128)(2,1)} %slice.277), channel_id=1, source_target_pairs={{0,192},{64,0},{128,64},{192,128},{1,193},{65,1},{129,65},{193,129... | collective-permute-start | bytes 3244040 | tf_op jit(solution)/shard_map/ppermute | solution.py:18
  160.9 39.2 %collective-permute-start.22 = (bf16[2,8,8,4224]{3,2,1,0:T(8,128)(2,1)}, bf16[2,8,8,4224]{3,2,1,0:T(8,128)(2,1)S(1)}, u32[]{:S(2)}, u32[]{:S(2)}) collective-permute-start(bf16[2,8,8,4224]{3,2,1,0:T(8,128)(2,1)} %slice.278), channel_id=1, source_target_pairs={{0,64},{64,128},{128,192},{192,0},{1,65},{65,129},{129,193},{193,1... | collective-permute-start | bytes 3244040 | tf_op jit(solution)/shard_map/ppermute | solution.py:18
  162.0 33.9 %collective-permute-start.23 = (bf16[2,8,8,4096]{3,2,1,0:T(8,128)(2,1)}, bf16[2,8,8,4096]{3,2,1,0:T(8,128)(2,1)S(1)}, u32[]{:S(2)}, u32[]{:S(2)}) collective-permute-start(bf16[2,8,8,4096]{3,2,1,0:T(8,128)(2,1)} %slice.279), channel_id=1, source_target_pairs={{0,48},{16,0},{32,16},{48,32},{1,49},{17,1},{33,17},{49,33},{2,50}... | collective-permute-start | bytes 3145736 | tf_op jit(solution)/shard_map/ppermute | solution.py:18
  166.6 32.8 %collective-permute-start.24 = (bf16[2,8,8,4096]{3,2,1,0:T(8,128)(2,1)}, bf16[2,8,8,4096]{3,2,1,0:T(8,128)(2,1)}, u32[]{:S(2)}, u32[]{:S(2)}) collective-permute-start(bf16[2,8,8,4096]{3,2,1,0:T(8,128)(2,1)} %slice.280), channel_id=1, source_target_pairs={{0,16},{16,32},{32,48},{48,0},{1,17},{17,33},{33,49},{49,1},{2,18}... | collective-permute-start | bytes 3145736 | tf_op jit(solution)/shard_map/ppermute | solution.py:18
  195.9 4.2 copy-start.12
  199.4 1.0 copy-start.10
  200.4 1.0 copy-start.11
  237.7 33.6 %collective-permute-start.25 = (bf16[2,8,8,4096]{3,2,1,0:T(8,128)(2,1)}, bf16[2,8,8,4096]{3,2,1,0:T(8,128)(2,1)S(1)}, u32[]{:S(2)}, u32[]{:S(2)}) collective-permute-start(bf16[2,8,8,4096]{3,2,1,0:T(8,128)(2,1)} %get-tuple-element.87), channel_id=1, source_target_pairs={{0,16},{16,32},{32,48},{48,0},{1,17},{17,33},{33,49},{49,1},{2,18}... | collective-permute-start | bytes 3145736 | tf_op jit(solution)/shard_map/ppermute | solution.py:18
  238.2 33.1 %collective-permute-start.26 = (bf16[2,8,8,4096]{3,2,1,0:T(8,128)(2,1)}, bf16[2,8,8,4096]{3,2,1,0:T(8,128)(2,1)}, u32[]{:S(2)}, u32[]{:S(2)}) collective-permute-start(bf16[2,8,8,4096]{3,2,1,0:T(8,128)(2,1)} %get-tuple-element.86), channel_id=1, source_target_pairs={{0,48},{16,0},{32,16},{48,32},{1,49},{17,1},{33,17},{49,33},{2,50}... | collective-permute-start | bytes 3145736 | tf_op jit(solution)/shard_map/ppermute | solution.py:18
  273.8 23.7 %collective-permute-start.28 = (bf16[2,8,8,4096]{3,2,1,0:T(8,128)(2,1)S(1)}, bf16[2,8,8,4096]{3,2,1,0:T(8,128)(2,1)S(1)}, u32[]{:S(2)}, u32[]{:S(2)}) collective-permute-start(bf16[2,8,8,4096]{3,2,1,0:T(8,128)(2,1)S(1)} %get-tuple-element.79), channel_id=1, source_target_pairs={{0,192},{64,0},{128,64},{192,128},{1,193},{65,1},{129,65},{193,129... | collective-permute-start | bytes 3145736 | tf_op jit(solution)/shard_map/ppermute | solution.py:18
  276.9 24.0 %collective-permute-start.27 = (bf16[2,8,8,4096]{3,2,1,0:T(8,128)(2,1)S(1)}, bf16[2,8,8,4096]{3,2,1,0:T(8,128)(2,1)S(1)}, u32[]{:S(2)}, u32[]{:S(2)}) collective-permute-start(bf16[2,8,8,4096]{3,2,1,0:T(8,128)(2,1)S(1)} %get-tuple-element.81), channel_id=1, source_target_pairs={{0,64},{64,128},{128,192},{192,0},{1,65},{65,129},{129,193},{193,1... | collective-permute-start | bytes 3145736 | tf_op jit(solution)/shard_map/ppermute | solution.py:18
  279.9 52.9 %collective-permute-start.35 = (bf16[4,8,8,4096]{3,2,1,0:T(8,128)(2,1)S(1)}, bf16[4,8,8,4096]{3,2,1,0:T(8,128)(2,1)S(1)}, u32[]{:S(2)}, u32[]{:S(2)}) collective-permute-start(bf16[4,8,8,4096]{3,2,1,0:T(8,128)(2,1)S(1)} %pad_maximum_fusion.7), channel_id=1, source_target_pairs={{0,16},{16,32},{32,48},{48,0},{1,17},{17,33},{33,49},{49,1},{2,18}... | collective-permute-start | bytes 6291464 | tf_op jit(solution)/shard_map/ppermute | solution.py:18
  280.3 52.5 %collective-permute-start.36 = (bf16[4,8,8,4096]{3,2,1,0:T(8,128)(2,1)S(1)}, bf16[4,8,8,4096]{3,2,1,0:T(8,128)(2,1)}, u32[]{:S(2)}, u32[]{:S(2)}) collective-permute-start(bf16[4,8,8,4096]{3,2,1,0:T(8,128)(2,1)S(1)} %pad_maximum_fusion.8), channel_id=1, source_target_pairs={{0,48},{16,0},{32,16},{48,32},{1,49},{17,1},{33,17},{49,33},{2,50}... | collective-permute-start | bytes 6291464 | tf_op jit(solution)/shard_map/ppermute | solution.py:18
  332.8 1.4 copy-start.13
  338.1 11.8 %copy-start.6 = (bf16[4,8,8,4096]{3,2,1,0:T(8,128)(2,1)}, bf16[4,8,8,4096]{3,2,1,0:T(8,128)(2,1)S(1)}, u32[]{:S(2)}) copy-start(bf16[4,8,8,4096]{3,2,1,0:T(8,128)(2,1)S(1)} %fusion.1) | copy-start | bytes 6291460
  339.0 10.7 %collective-permute-start.37 = (bf16[4,8,4096]{2,1,0:T(8,128)(2,1)}, bf16[4,8,4096]{2,1,0:T(8,128)(2,1)S(1)}, u32[]{:S(2)}, u32[]{:S(2)}) collective-permute-start(bf16[4,8,4096]{2,1,0:T(8,128)(2,1)} %get-tuple-element.104), channel_id=1, source_target_pairs={{0,64},{64,128},{128,192},{192,0},{1,65},{65,129},{129,193},{193,1... | collective-permute-start | bytes 786440 | tf_op jit(solution)/shard_map/ppermute | solution.py:18
  339.0 10.7 %collective-permute-start.39 = (bf16[4,8,4096]{2,1,0:T(8,128)(2,1)S(1)}, bf16[4,8,4096]{2,1,0:T(8,128)(2,1)S(1)}, u32[]{:S(2)}, u32[]{:S(2)}) collective-permute-start(bf16[4,8,4096]{2,1,0:T(8,128)(2,1)S(1)} %get-tuple-element.105), channel_id=1, source_target_pairs={{0,192},{64,0},{128,64},{192,128},{1,193},{65,1},{129,65},{193,129... | collective-permute-start | bytes 786440 | tf_op jit(solution)/shard_map/ppermute | solution.py:18
  342.3 51.8 %collective-permute-start.30 = (bf16[4,8,8,4096]{3,2,1,0:T(8,128)(2,1)}, bf16[4,8,8,4096]{3,2,1,0:T(8,128)(2,1)}, u32[]{:S(2)}, u32[]{:S(2)}) collective-permute-start(bf16[4,8,8,4096]{3,2,1,0:T(8,128)(2,1)} %get-tuple-element.65), channel_id=1, source_target_pairs={{0,192},{64,0},{128,64},{192,128},{1,193},{65,1},{129,65},{193,129... | collective-permute-start | bytes 6291464 | tf_op jit(solution)/shard_map/ppermute | solution.py:18
  342.3 52.4 %collective-permute-start.29 = (bf16[4,8,8,4096]{3,2,1,0:T(8,128)(2,1)}, bf16[4,8,8,4096]{3,2,1,0:T(8,128)(2,1)}, u32[]{:S(2)}, u32[]{:S(2)}) collective-permute-start(bf16[4,8,8,4096]{3,2,1,0:T(8,128)(2,1)} %get-tuple-element.64), channel_id=1, source_target_pairs={{0,64},{64,128},{128,192},{192,0},{1,65},{65,129},{129,193},{193,1... | collective-permute-start | bytes 6291464 | tf_op jit(solution)/shard_map/ppermute | solution.py:18
  344.3 148.0 %collective-permute-start.41 = (bf16[3,192,4096]{2,1,0:T(8,128)(2,1)}, bf16[3,192,4096]{2,1,0:T(8,128)(2,1)}, u32[]{:S(2)}, u32[]{:S(2)}) collective-permute-start(bf16[3,192,4096]{2,1,0:T(8,128)(2,1)} %get-tuple-element.77), channel_id=1, source_target_pairs={{0,1},{1,0},{2,3},{3,2},{4,5},{5,4},{6,7},{7,6},{8,9},{9,8},{10,11... | collective-permute-start | bytes 14155784 | tf_op jit(solution)/shard_map/ppermute | solution.py:18
  349.9 52.0 %collective-permute-start.40 = (bf16[8,8,4096]{2,1,0:T(8,128)(2,1)S(1)}, bf16[8,8,4096]{2,1,0:T(8,128)(2,1)S(1)}, u32[]{:S(2)}, u32[]{:S(2)}) collective-permute-start(bf16[8,8,4096]{2,1,0:T(8,128)(2,1)S(1)} %pad_maximum_fusion.12), channel_id=1, source_target_pairs={{0,192},{64,0},{128,64},{192,128},{1,193},{65,1},{129,65},{193,129... | collective-permute-start | bytes 1572872 | tf_op jit(solution)/shard_map/ppermute | solution.py:18
  353.0 48.8 %collective-permute-start.38 = (bf16[8,8,4096]{2,1,0:T(8,128)(2,1)S(1)}, bf16[8,8,4096]{2,1,0:T(8,128)(2,1)S(1)}, u32[]{:S(2)}, u32[]{:S(2)}) collective-permute-start(bf16[8,8,4096]{2,1,0:T(8,128)(2,1)S(1)} %pad_maximum_fusion.11), channel_id=1, source_target_pairs={{0,64},{64,128},{128,192},{192,0},{1,65},{65,129},{129,193},{193,1... | collective-permute-start | bytes 1572872 | tf_op jit(solution)/shard_map/ppermute | solution.py:18
  398.8 8.3 %collective-permute-start.31 = (bf16[4,8,4096]{2,1,0:T(8,128)(2,1)S(1)}, bf16[4,8,4096]{2,1,0:T(8,128)(2,1)S(1)}, u32[]{:S(2)}, u32[]{:S(2)}) collective-permute-start(bf16[4,8,4096]{2,1,0:T(8,128)(2,1)S(1)} %get-tuple-element.98), channel_id=1, source_target_pairs={{0,16},{16,32},{32,48},{48,0},{1,17},{17,33},{33,49},{49,1},{2,18}... | collective-permute-start | bytes 786440 | tf_op jit(solution)/shard_map/ppermute | solution.py:18
  400.1 8.9 %collective-permute-start.33 = (bf16[4,8,4096]{2,1,0:T(8,128)(2,1)S(1)}, bf16[4,8,4096]{2,1,0:T(8,128)(2,1)S(1)}, u32[]{:S(2)}, u32[]{:S(2)}) collective-permute-start(bf16[4,8,4096]{2,1,0:T(8,128)(2,1)S(1)} %get-tuple-element.100), channel_id=1, source_target_pairs={{0,48},{16,0},{32,16},{48,32},{1,49},{17,1},{33,17},{49,33},{2,50}... | collective-permute-start | bytes 786440 | tf_op jit(solution)/shard_map/ppermute | solution.py:18
  410.0 9.9 %collective-permute-start.34 = (bf16[8,8,4096]{2,1,0:T(8,128)(2,1)}, bf16[8,8,4096]{2,1,0:T(8,128)(2,1)S(1)}, u32[]{:S(2)}, u32[]{:S(2)}) collective-permute-start(bf16[8,8,4096]{2,1,0:T(8,128)(2,1)} %pad_maximum_fusion.10), channel_id=1, source_target_pairs={{0,48},{16,0},{32,16},{48,32},{1,49},{17,1},{33,17},{49,33},{2,50}... | collective-permute-start | bytes 1572872 | tf_op jit(solution)/shard_map/ppermute | solution.py:18
  413.6 11.1 %collective-permute-start.32 = (bf16[8,8,4096]{2,1,0:T(8,128)(2,1)}, bf16[8,8,4096]{2,1,0:T(8,128)(2,1)S(1)}, u32[]{:S(2)}, u32[]{:S(2)}) collective-permute-start(bf16[8,8,4096]{2,1,0:T(8,128)(2,1)} %pad_maximum_fusion.9), channel_id=1, source_target_pairs={{0,16},{16,32},{32,48},{48,0},{1,17},{17,33},{33,49},{49,1},{2,18}... | collective-permute-start | bytes 1572872 | tf_op jit(solution)/shard_map/ppermute | solution.py:18
  414.6 76.2 %reduce-scatter.3.cloned.1.call-start = ((), (), s32[]{:S(2)}) async-start(), calls=%async_computation.3 | async-start | bytes 589824 | tf_op jit(solution)/shard_map/reduce_scatter | solution.py:351
Sparse Core Ops, SparseCore 0:
  11.9 198.5 all-gather.1
  414.7 36.8 reduce-scatter.4
  454.8 35.8 reduce-scatter.2
where the time goes:
time: 517 us; the launch traced here: 508 us
  waiting for transfers between devices  271 us (52%)
  Pallas kernels  90.5 us (18%)
  starting transfers between devices  63.7 us (12%)
  other arithmetic  43.8 us (8%)
  local copies, waits for them, and re-layouts  24.4 us (5%)
  between operations  14.7 us (3%)
    ppermute x42, waiting for transfers between devices, shift(): lax.ppermute(value, axis, [(i, (i + by) % size) for i in range(size)])  206 us
    reduce_scatter x2, waiting for transfers between devices, on_device(): lax.psum_scatter(r.reshape(nz * half, width), 'z', scatter_dimension=0, t...  65.1 us
    ppermute x42, starting transfers between devices, shift(): lax.ppermute(value, axis, [(i, (i + by) % size) for i in range(size)])  63.6 us
    pallas_call x1, Pallas kernels, second_call(): pl.pallas_call(second_kernel, grid_spec=pltpu.PrefetchScalarGridSpec(num_...  32.4 us
    pallas_call x1, Pallas kernels, first_call(): pl.pallas_call(first_kernel, grid_spec=pltpu.PrefetchScalarGridSpec(num_s...  31 us
    pallas_call x1, Pallas kernels, weight_call(): pl.pallas_call(weight_kernel, grid_spec=pltpu.PrefetchScalarGridSpec(num_...  27.2 us
    convert_element_type x7, other arithmetic, add(): return total.astype(BF16)  14.2 us
    concatenate x1, other arithmetic, on_device(): wgu = jnp.concatenate([w_gate[0], swapped[0], w_up[0], swapped[1]], axis=0)  11.1 us
  transfers between devices with their start and end apart: 45, of which 28 were waited for; matrix products, arithmetic and copies ran while one was open for 8% of the time, Pallas kernels for 18%

commit v1 on v0

--- a/solution.py
+++ b/solution.py
@@ -41,9 +41,15 @@
     return near, back
 
 
-def ring_sum4(own, near, opposite, back, axis):
-    near, back = ring_middle4(near, back, ring_ends4(opposite, axis))
-    return add(own, *ring_ends(near, back, axis))
+def direct_sum(blocks, axis):
+    size, far = len(blocks), len(blocks) // 2
+    half = blocks[far].shape[0] // 2
+    moved = [shift(b, axis, k if k < far else k - size) for k, b in enumerate(blocks) if k not in (0, far)]
+    up, down = shift(blocks[far][:half], axis, far), shift(blocks[far][half:], axis, -far)
+    total = blocks[0].astype(F32)
+    for block in moved:
+        total = total + block.astype(F32)
+    return (total + jnp.concatenate([up, down], axis=0).astype(F32)).astype(BF16)
 
 
 def ring_gather4(first, first_axis, second, second_axis, beside=()):
@@ -105,17 +111,18 @@
     expert_terms(ids, flat(t_ref), flat(g_ref), flat(m_ref), wgu_ref, wd_ref, p_ref, dgu_ref, h_ref)
 
 
-def first_call(ids, rows, wgu, wd, lanes):
+def first_call(ids, rows, wgu, wd, lanes, start, stop, stride):
     nx, ny, nz, _, _, half, _ = rows.shape
     width = wgu.shape[1]
     hid = wd.shape[0]
     count = ny * nz * half
-    at = lambda i, ids: lax.rem(ids[0] + i, nx)
+    steps = len(range(start, stop, stride))
+    at = lambda i, ids: lax.rem(ids[0] + start + i * stride, nx)
     return pl.pallas_call(
         first_kernel,
         grid_spec=pltpu.PrefetchScalarGridSpec(
             num_scalar_prefetch=1,
-            grid=(nx,),
+            grid=(steps,),
             in_specs=[
                 pl.BlockSpec((1, ny, nz, 1, 1, half, width), lambda i, ids: (at(i, ids), 0, 0, ids[2], 0, 0, 0)),
                 pl.BlockSpec((1, ny, nz, 1, 1, half, width), lambda i, ids: (at(i, ids), 0, 0, ids[2], 1, 0, 0)),
@@ -127,17 +134,17 @@
             ],
             out_specs=[
                 pl.BlockSpec((1, ny, nz, half, width), lambda i, ids: (i, 0, 0, 0, 0)),
-                pl.BlockSpec((1, 2 * hid, count), lambda i, ids: (at(i, ids), 0, 0)),
-                pl.BlockSpec((1, hid, count), lambda i, ids: (at(i, ids), 0, 0)),
+                pl.BlockSpec((1, 2 * hid, count), lambda i, ids: (i, 0, 0)),
+                pl.BlockSpec((1, hid, count), lambda i, ids: (i, 0, 0)),
             ],
         ),
         out_shape=[
-            jax.ShapeDtypeStruct((nx, ny, nz, half, width), BF16),
-            jax.ShapeDtypeStruct((nx, 2 * hid, count), BF16),
-            jax.ShapeDtypeStruct((nx, hid, count), BF16),
+            jax.ShapeDtypeStruct((steps, ny, nz, half, width), BF16),
+            jax.ShapeDtypeStruct((steps, 2 * hid, count), BF16),
+            jax.ShapeDtypeStruct((steps, hid, count), BF16),
         ],
         compiler_params=pltpu.CompilerParams(vmem_limit_bytes=56 << 20),
-        name="tokens_first",
+        name=f"tokens_first{start}",
     )(ids, rows, rows, rows, wgu, wd)
 
 
@@ -221,9 +228,10 @@
 def weight_kernel(ids, *refs):
     t_ref, g_ref = refs[:2]
     t_parts, g_parts = refs[2:7], refs[7:12]
-    dgu0_ref, dgu1_ref, h0_ref, h1_ref, mine_ref, other_ref = refs[12:]
+    dgu0_refs, h0_refs = refs[12:15], refs[15:18]
+    dgu1_ref, h1_ref, mine_ref, other_ref = refs[18:]
     nx, ny, nz, _, _, half, tile = t_ref.shape
-    unit = h0_ref.shape[1] // 2
+    unit = h1_ref.shape[1] // 2
     flat = lambda a: a.reshape(-1, tile)
 
     def by_x(i):
@@ -240,17 +248,19 @@
                 pieces.append(flat(g_parts[2][i] if i < nx // 2 else g_parts[3][i - nx // 2]))
         return jnp.concatenate(pieces, axis=0)
 
-    def outer(first, second, ref, right):
+    def outer(first, second, ref, later):
         total = None
+        blocks = first[0][0], first[1][0], first[2][0], first[1][1]
         for i in range(nx):
-            term = jnp.dot(first[i], flat(ref[i, :, :, 0, 0]), preferred_element_type=F32)
+            right = flat(ref[lax.rem(ids[0] + i, nx), :, :, 0, 0])
+            term = jnp.dot(blocks[i], right, preferred_element_type=F32)
             total = term if total is None else total + term
         for i in range(nx):
-            total = total + jnp.dot(second[i], right(i), preferred_element_type=F32)
+            total = total + jnp.dot(second[i], later(i), preferred_element_type=F32)
         return total
 
-    gu = outer(dgu0_ref, dgu1_ref, t_ref, by_x)
-    down = outer(h0_ref, h1_ref, g_ref, across)
+    gu = outer(dgu0_refs, dgu1_ref, t_ref, by_x)
+    down = outer(h0_refs, h1_ref, g_ref, across)
     mine_ref[0] = gu[:unit]
     mine_ref[1] = gu[2 * unit : 3 * unit]
     mine_ref[2] = down[:unit]
@@ -262,7 +272,7 @@
 def weight_call(ids, rows, t_parts, g_parts, dgu0, dgu1, h0, h1):
     nx, ny, nz, _, _, half, _ = rows.shape
     width = g_parts[0].shape[-1]
-    unit = h0.shape[1] // 2
+    unit = h1.shape[1] // 2
     tile = 512
     whole = lambda a: pl.BlockSpec(a.shape, lambda j, ids: (0, 0, 0), pipeline_mode=pl.Buffered(1))
     part = lambda a: pl.BlockSpec((*a.shape[:3], tile), lambda j, ids: (0, 0, 0, j))
@@ -276,10 +286,7 @@
                 pl.BlockSpec((nx, ny, nz, 1, 1, half, tile), lambda j, ids: (0, 0, 0, ids[2], 1, 0, j)),
                 *(part(a) for a in t_parts),
                 *(part(a) for a in g_parts),
-                whole(dgu0),
-                whole(dgu1),
-                whole(h0),
-                whole(h1),
+                *(whole(a) for a in (*dgu0, *h0, dgu1, h1)),
             ],
             out_specs=[
                 pl.BlockSpec((3, unit, tile), lambda j, ids: (0, 0, j)),
@@ -292,7 +299,7 @@
         ],
         compiler_params=pltpu.CompilerParams(vmem_limit_bytes=56 << 20),
         name="weights",
-    )(ids, rows, rows, *t_parts, *g_parts, dgu0, dgu1, h0, h1)
+    )(ids, rows, rows, *t_parts, *g_parts, *dgu0, *h0, dgu1, h1)
 
 
 def pick_weights(routes, router_weights, experts):
@@ -332,26 +339,30 @@
     p1, dgu1, h1 = second_call(ids, t_parts, g_parts, wgu, wd)
     ends1 = ring_ends4(p1[2], "y")
     rows, dgu1 = lax.optimization_barrier((rows, dgu1))
-    p0, dgu0, h0 = first_call(ids, rows, wgu, wd, lanes)
-    ends1, p0, dgu0, h0 = lax.optimization_barrier((ends1, p0, dgu0, h0))
-    ends0 = ring_ends4(p0[2], "x")
-    near1, back1 = ring_middle4(p1[1], p1[3], ends1)
-    last1 = ring_ends(near1, back1, "y")
-    near0, back0 = ring_middle4(p0[1], p0[3], ends0)
-    near0, back0, dgu0 = lax.optimization_barrier((near0, back0, dgu0))
+    first = functools.partial(first_call, ids, wgu=wgu, wd=wd, lanes=lanes)
+    p_far, dgu_far, h_far = first(rows, start=2, stop=3, stride=1)
+    ends1, p_far, rows = lax.optimization_barrier((ends1, p_far, rows))
+    ends0 = ring_ends4(p_far[0], "x")
+    last1 = ring_ends(*ring_middle4(p1[1], p1[3], ends1), "y")
+    p_side, dgu_side, h_side = first(rows, start=1, stop=4, stride=2)
+    ends0, p_side, rows = lax.optimization_barrier((ends0, p_side, rows))
+    near0, back0 = ring_middle4(p_side[0], p_side[1], ends0)
     last0 = ring_ends(near0, back0, "x")
-    mine, other = weight_call(ids, rows, t_parts, g_parts, dgu0, dgu1, h0, h1)
-    last1, mine, other = lax.optimization_barrier((last1, mine, other))
+    near0, rows = lax.optimization_barrier((near0, rows))
+    p_own, dgu_own, h_own = first(rows, start=0, stop=1, stride=1)
+    mine, other = weight_call(
+        ids, rows, t_parts, g_parts, (dgu_own, dgu_side, dgu_far), dgu1, (h_own, h_side, h_far), h1
+    )
+    last1, other = lax.optimization_barrier((last1, other))
+    last0, mine = lax.optimization_barrier((last0, mine))
+    grads = (mine + shift(other, "c", 1).astype(F32)).astype(BF16)
     q1 = add(p1[0], *last1)
-    r1 = ring_sum4(q1[0], q1[1], q1[2], q1[3], "x")
+    r1 = direct_sum([q1[k] for k in range(nx)], "x")
     r1 = lax.dynamic_slice_in_dim(jnp.concatenate([r1, r1], axis=0), nz - iz, nz, axis=0)
-    q0 = add(p0[0], *last0)
-    pick = lambda k: lax.dynamic_index_in_dim(q0, lax.rem(iy + k, ny), 0, keepdims=False)
-    r0 = ring_sum4(pick(0), pick(1), pick(2), pick(3), "y")
-    scatter = lambda r: lax.psum_scatter(r.reshape(nz * half, width), "z", scatter_dimension=0, tiled=True)
-    grad_tokens = jnp.concatenate([scatter(r0), scatter(r1)], axis=0)
-
-    grads = (mine + shift(other, "c", 1).astype(F32)).astype(BF16)
+    q0 = add(p_own[0], *last0)
+    r0 = direct_sum([lax.dynamic_index_in_dim(q0, lax.rem(iy + k, ny), 0, keepdims=False) for k in range(ny)], "y")
+    both = jnp.concatenate([r0, r1], axis=1).reshape(nz * per, width)
+    grad_tokens = lax.psum_scatter(both, "z", scatter_dimension=0, tiled=True)
     return grad_tokens, grads[0:1], grads[1:2], grads[2:3]
 
 

time: 517 us -> 460 us (0.89)
  waiting for transfers between devices: 271 us -> 206 us
  Pallas kernels: 90.5 us -> 104 us
    reduce_scatter x2 -> x1, waiting for transfers between devices: 65.1 us -> 27.9 us  [on_device(): grad_tokens = lax.psum_scatter(both, 'z', scatter_dimension=0, tiled=True)]
    ppermute x42, waiting for transfers between devices: 206 us -> 178 us  [shift(): lax.ppermute(value, axis, [(i, (i + by) % size) for i in range(size)])]
    pallas_call x1 -> x3, Pallas kernels: 31 us -> 44.8 us  [first_call(): pl.pallas_call(first_kernel, grid_spec=pltpu.PrefetchScalarGridSpec(num_s...]
    convert_element_type x7 -> x4, other arithmetic: 14.2 us -> 11.5 us  [add(): return total.astype(BF16)]
  transfers between devices with their start and end apart: 45 -> 44, of which waited for: 28 -> 26; matrix products, arithmetic and copies ran while one was open for 8% -> 12% of each run, Pallas kernels for 18% -> 23%
where the time goes in v1:
time: 460 us; the launch traced here: 451 us
  waiting for transfers between devices  206 us (45%)
  Pallas kernels  104 us (23%)
  starting transfers between devices  60.1 us (13%)
  other arithmetic  39.2 us (9%)
  local copies, waits for them, and re-layouts  26.3 us (6%)
  between operations  14.9 us (3%)
    ppermute x42, waiting for transfers between devices, shift(): lax.ppermute(value, axis, [(i, (i + by) % size) for i in range(size)])  178 us
    ppermute x42, starting transfers between devices, shift(): lax.ppermute(value, axis, [(i, (i + by) % size) for i in range(size)])  60 us
    pallas_call x3, Pallas kernels, first_call(): pl.pallas_call(first_kernel, grid_spec=pltpu.PrefetchScalarGridSpec(num_s...  44.8 us
    pallas_call x1, Pallas kernels, second_call(): pl.pallas_call(second_kernel, grid_spec=pltpu.PrefetchScalarGridSpec(num_...  32 us
    reduce_scatter x1, waiting for transfers between devices, on_device(): grad_tokens = lax.psum_scatter(both, 'z', scatter_dimension=0, tiled=True)  27.9 us
    pallas_call x1, Pallas kernels, weight_call(): pl.pallas_call(weight_kernel, grid_spec=pltpu.PrefetchScalarGridSpec(num_...  27.3 us
    convert_element_type x4, other arithmetic, add(): return total.astype(BF16)  11.5 us
    concatenate x1, other arithmetic, on_device(): wgu = jnp.concatenate([w_gate[0], swapped[0], w_up[0], swapped[1]], axis=0)  11.1 us
  transfers between devices with their start and end apart: 44, of which 26 were waited for; matrix products, arithmetic and copies ran while one was open for 12% of the time, Pallas kernels for 23%

profile of v1, /device:TPU:8, one launch (start us, length us, event | category | flops | bytes accessed | tf_op | source)
XLA Modules:
  0.0 450.6 jit_solution(11303994743663618196)
XLA Ops:
  11.5 5.9 %collective-permute-start = (bf16[8,8320]{1,0:T(8,128)(2,1)S(1)}, bf16[8,8320]{1,0:T(8,128)(2,1)S(1)}, u32[]{:S(2)}, u32[]{:S(2)}) collective-permute-start(bf16[8,8320]{1,0:T(8,128)(2,1)S(1)} %pad_maximum_fusion.10), channel_id=1, source_target_pairs={{0,14},{2,0},{4,2},{6,4},{8,6},{10,8},{12,10},{14,12},{1,15},{3,1}... | collective-permute-start | bytes 399368 | tf_op jit(solution)/shard_map/ppermute | solution.py:18
  18.3 1.9 collective-permute-done
  20.2 3.7 collective-permute-start.1
  24.0 2.5 collective-permute-done.1
  26.5 3.7 collective-permute-start.2
  30.2 2.5 collective-permute-done.2
  32.7 3.7 collective-permute-start.3
  36.5 5.5 %collective-permute-done.9 = bf16[8,4096]{1,0:T(8,128)(2,1)S(1)} collective-permute-done((bf16[8,4096]{1,0:T(8,128)(2,1)S(1)}, bf16[8,4096]{1,0:T(8,128)(2,1)S(1)}, u32[]{:S(2)}, u32[]{:S(2)}) %collective-permute-start.9) | collective-permute-done | bytes 65568 | tf_op jit(solution)/shard_map/ppermute | solution.py:18
  42.7 1.5 collective-permute-start.8
  44.2 3.0 collective-permute-start.10
  47.2 8.2 %collective-permute-done.10 = bf16[8,8,4096]{2,1,0:T(8,128)(2,1)S(1)} collective-permute-done((bf16[8,8,4096]{2,1,0:T(8,128)(2,1)S(1)}, bf16[8,8,4096]{2,1,0:T(8,128)(2,1)S(1)}, u32[]{:S(2)}, u32[]{:S(2)}) %collective-permute-start.10) | collective-permute-done | bytes 524320 | tf_op jit(solution)/shard_map/ppermute | solution.py:18
  55.5 3.8 collective-permute-done.11
  59.4 2.1 collective-permute-start.15
  62.2 1.7 collective-permute-start.13
  63.9 1.8 collective-permute-done.14
  65.7 1.3 collective-permute-done.15
  67.4 1.9 collective-permute-done.12
  69.3 2.0 collective-permute-done.13
  74.4 2.9 collective-permute-start.16
  77.3 3.2 collective-permute-start.18
  80.5 1.9 collective-permute-done.20
  82.8 1.8 pad_maximum_fusion.2.refs_11_.wd_ref
  84.7 11.1 %pad_maximum_fusion.refs_10_.wgu_ref = bf16[768,4096]{1,0:T(8,128)(2,1)} fusion(bf16[192,4096]{1,0:T(8,128)(2,1)S(1)} %get-tuple-element.106, bf16[192,4096]{1,0:T(8,128)(2,1)S(1)} %bitcast.147, bf16[192,4096]{1,0:T(8,128)(2,1)S(1)} %get-tuple-element.107, bf16[192,4096]{1,0:T(8,128)(2,1)S(1)} %bitcast.148), kind=kLoop, calls=%fused_computation.1 | loop fusion | flops 25165824 | bytes 12582912 | tf_op jit(solution)/shard_map/concatenate | solution.py:335
  95.8 49.7 %collective-permute-done.18.refs_6_.refs_8_ = bf16[4,8,8,4096]{3,2,1,0:T(8,128)(2,1)S(1)} collective-permute-done((bf16[4,8,8,4096]{3,2,1,0:T(8,128)(2,1)S(1)}, bf16[4,8,8,4096]{3,2,1,0:T(8,128)(2,1)S(1)}, u32[]{:S(2)}, u32[]{:S(2)}) %collective-permute-start.18) | collective-permute-done | bytes 2097184 | tf_op jit(solution)/shard_map/ppermute | solution.py:18
  145.4 3.4 collective-permute-done.19.refs_9_.refs_11_
  150.3 1.1 slice.231
  151.4 2.9 collective-permute-start.21
  156.4 2.6 collective-permute-start.23
  159.1 1.1 slice.234
  161.2 34.3 %collective-permute-done.23.refs_7_.refs_9_ = bf16[2,8,8,4096]{3,2,1,0:T(8,128)(2,1)S(1)} collective-permute-done((bf16[2,8,8,4096]{3,2,1,0:T(8,128)(2,1)}, bf16[2,8,8,4096]{3,2,1,0:T(8,128)(2,1)S(1)}, u32[]{:S(2)}, u32[]{:S(2)}) %collective-permute-start.23) | collective-permute-done | bytes 1048608 | tf_op jit(solution)/shard_map/ppermute | solution.py:18
  195.5 1.3 collective-permute-done.24.refs_8_.refs_10_
  197.7 1.9 collective-permute-done.22.refs_3_.refs_5_
  200.5 32.0 %tokens_second.1 = (bf16[4,4,8,8,4096]{4,3,2,1,0:T(8,128)(2,1)}, bf16[4,768,256]{2,1,0:T(8,128)(2,1)}, bf16[4,384,256]{2,1,0:T(8,128)(2,1)}) custom-call(s32[5]{0:T(128)} %stack.107.ids, bf16[4,8,8,4224]{3,2,1,0:T(8,128)(2,1)} %copy-done, bf16[4,8,8,4224]{3,2,1,0:T(8,128)(2,1)} %copy-done.2, bf16[2,8,8,4224]{3,2,1,0:T(8,128)(2,1)} %copy-done.9, ...), custom_call_target="tpu_custom_call" | custom-call | tf_op jit(solution)/shard_map/tokens_second/pallas_call | solution.py:197
  232.5 3.9 slice_bitcast_fusion.3
  236.5 1.1 collective-permute-start.25
  238.5 12.8 %tokens_first2.1 = (bf16[1,4,8,8,4096]{4,3,2,1,0:T(8,128)(2,1)}, bf16[1,768,256]{2,1,0:T(8,128)(2,1)}, bf16[1,384,256]{2,1,0:T(8,128)(2,1)}) custom-call(s32[5]{0:T(128)} %stack.107.ids, bf16[4,4,8,2,2,8,4224]{6,5,4,3,2,1,0:T(8,128)(2,1)} %bitcast.136, bf16[4,4,8,2,2,8,4224]{6,5,4,3,2,1,0:T(8,128)(2,1)} %bitcast.137, ...), custom_call_target="tpu_custom_call" | custom-call | tf_op jit(solution)/shard_map/tokens_first2/pallas_call | solution.py:121
  251.3 10.4 %collective-permute-done.25 = bf16[2,8,8,4096]{3,2,1,0:T(8,128)(2,1)S(1)} collective-permute-done((bf16[2,8,8,4096]{3,2,1,0:T(8,128)(2,1)}, bf16[2,8,8,4096]{3,2,1,0:T(8,128)(2,1)S(1)}, u32[]{:S(2)}, u32[]{:S(2)}) %collective-permute-start.25) | collective-permute-done | bytes 1048608 | tf_op jit(solution)/shard_map/ppermute | solution.py:18
  262.3 3.1 slice_bitcast_fusion.7
  265.6 3.2 collective-permute-start.28
  268.8 2.6 fusion.4
  271.4 19.3 %tokens_first1.1 = (bf16[2,4,8,8,4096]{4,3,2,1,0:T(8,128)(2,1)}, bf16[2,768,256]{2,1,0:T(8,128)(2,1)}, bf16[2,384,256]{2,1,0:T(8,128)(2,1)}) custom-call(s32[5]{0:T(128)} %stack.107.ids, bf16[4,4,8,2,2,8,4224]{6,5,4,3,2,1,0:T(8,128)(2,1)} %bitcast.139, bf16[4,4,8,2,2,8,4224]{6,5,4,3,2,1,0:T(8,128)(2,1)} %bitcast.140, ...), custom_call_target="tpu_custom_call" | custom-call | tf_op jit(solution)/shard_map/tokens_first1/pallas_call | solution.py:121
  290.9 2.4 collective-permute-start.36
  293.6 1.9 copy-done.12
  295.7 2.4 fusion.6
  298.1 1.5 pad_maximum_fusion.6
  300.5 1.6 pad_maximum_fusion.5
  302.1 1.3 collective-permute-start.29
  303.4 12.7 %tokens_first0.1 = (bf16[1,4,8,8,4096]{4,3,2,1,0:T(8,128)(2,1)}, bf16[1,768,256]{2,1,0:T(8,128)(2,1)}, bf16[1,384,256]{2,1,0:T(8,128)(2,1)}) custom-call(s32[5]{0:T(128)} %stack.107.ids, bf16[4,4,8,2,2,8,4224]{6,5,4,3,2,1,0:T(8,128)(2,1)} %bitcast.142, bf16[4,4,8,2,2,8,4224]{6,5,4,3,2,1,0:T(8,128)(2,1)} %bitcast.143, ...), custom_call_target="tpu_custom_call" | custom-call | tf_op jit(solution)/shard_map/tokens_first0/pallas_call | solution.py:121
  316.1 27.3 %weights.1 = (f32[3,192,4096]{2,1,0:T(8,128)}, bf16[3,192,4096]{2,1,0:T(8,128)(2,1)}) custom-call(s32[5]{0:T(128)} %stack.107.ids, bf16[4,4,8,2,2,8,4224]{6,5,4,3,2,1,0:T(8,128)(2,1)} %bitcast.145, bf16[4,4,8,2,2,8,4224]{6,5,4,3,2,1,0:T(8,128)(2,1)} %bitcast.146, bf16[4,8,8,4224]{3,2,1,0:T(8,128)(2,1)} %copy-done, bf16[4,8,8,4224]{3,2,1,0:T(8,128)(2,1)} %copy-done.2, ...), custom_call_target="tpu_custom_call" | custom-call | tf_op jit(solution)/shard_map/weights/pallas_call | solution.py:279
  343.4 3.3 fusion.1
  349.0 2.4 collective-permute-start.37
  352.3 5.9 %collective-permute-done.39 = bf16[4,8,4096]{2,1,0:T(8,128)(2,1)S(1)} collective-permute-done((bf16[4,8,4096]{2,1,0:T(8,128)(2,1)S(1)}, bf16[4,8,4096]{2,1,0:T(8,128)(2,1)S(1)}, u32[]{:S(2)}, u32[]{:S(2)}) %collective-permute-start.39) | collective-permute-done | bytes 262176 | tf_op jit(solution)/shard_map/ppermute | solution.py:18
  358.8 13.0 %collective-permute-done.40 = bf16[4,8,4096]{2,1,0:T(8,128)(2,1)} collective-permute-done((bf16[4,8,4096]{2,1,0:T(8,128)(2,1)}, bf16[4,8,4096]{2,1,0:T(8,128)(2,1)}, u32[]{:S(2)}, u32[]{:S(2)}) %collective-permute-start.40) | collective-permute-done | bytes 262176 | tf_op jit(solution)/shard_map/ppermute | solution.py:18
  371.8 1.2 fusion.10
  373.0 3.3 fusion.3
  376.7 2.8 collective-permute-start.32
  379.6 2.1 collective-permute-start.33
  381.7 1.5 collective-permute-start.34
  383.4 16.4 %collective-permute-done.33 = bf16[4,8,4096]{2,1,0:T(8,128)(2,1)S(1)} collective-permute-done((bf16[4,8,4096]{2,1,0:T(8,128)(2,1)S(1)}, bf16[4,8,4096]{2,1,0:T(8,128)(2,1)S(1)}, u32[]{:S(2)}, u32[]{:S(2)}) %collective-permute-start.33) | collective-permute-done | bytes 262176 | tf_op jit(solution)/shard_map/ppermute | solution.py:18
  399.8 5.2 %collective-permute-done.34 = bf16[4,8,4096]{2,1,0:T(8,128)(2,1)S(1)} collective-permute-done((bf16[4,8,4096]{2,1,0:T(8,128)(2,1)S(1)}, bf16[4,8,4096]{2,1,0:T(8,128)(2,1)S(1)}, u32[]{:S(2)}, u32[]{:S(2)}) %collective-permute-start.34) | collective-permute-done | bytes 262176 | tf_op jit(solution)/shard_map/ppermute | solution.py:18
  405.3 1.1 pad_maximum_fusion.9
  406.4 6.6 %add_convert_fusion = bf16[3,192,4096]{2,1,0:T(8,128)(2,1)S(1)} fusion(f32[3,192,4096]{2,1,0:T(8,128)} %get-tuple-element.94, bf16[3,192,4096]{2,1,0:T(8,128)(2,1)} %collective-permute-done.41), kind=kLoop, calls=%fused_computation | loop fusion | flops 7077888 | bytes 18874368 | tf_op jit(solution)/shard_map/convert_element_type | solution.py:358
  413.0 2.3 fusion.28
  415.4 27.9 %reduce-scatter.2.cloned.1.call-done = bf16[16,4096]{1,0:T(8,128)(2,1)} async-done(((bf16[128,4096]{1,0:T(8,128)(2,1)}), bf16[16,4096]{1,0:T(8,128)(2,1)}) %reduce-scatter.2.cloned.1.call-update) | async-done | bytes 131088 | tf_op jit(solution)/shard_map/reduce_scatter | solution.py:365
  (124 shorter events, 25.2 us)
Async XLA Ops:
  7.2 231.3 %all-gather.2.cloned.1.call-start = ((), (), s32[]{:S(2)}) async-start(), calls=%async_computation.1 | async-start | bytes 34738176 | tf_op jit(solution)/shard_map/all_gather | solution.py:325
  11.4 431.8 %reduce-scatter.2.cloned.1.call-start = ((), (), s32[]{:S(2)}) async-start(), calls=%async_computation.2 | async-start | bytes 1179648 | tf_op jit(solution)/shard_map/reduce_scatter | solution.py:365
  11.5 8.7 %collective-permute-start = (bf16[8,8320]{1,0:T(8,128)(2,1)S(1)}, bf16[8,8320]{1,0:T(8,128)(2,1)S(1)}, u32[]{:S(2)}, u32[]{:S(2)}) collective-permute-start(bf16[8,8320]{1,0:T(8,128)(2,1)S(1)} %pad_maximum_fusion.10), channel_id=1, source_target_pairs={{0,14},{2,0},{4,2},{6,4},{8,6},{10,8},{12,10},{14,12},{1,15},{3,1}... | collective-permute-start | bytes 399368 | tf_op jit(solution)/shard_map/ppermute | solution.py:18
  17.4 6.5 %collective-permute-start.4 = (bf16[8,8320]{1,0:T(8,128)(2,1)S(1)}, bf16[8,8320]{1,0:T(8,128)(2,1)S(1)}, u32[]{:S(2)}, u32[]{:S(2)}) collective-permute-start(bf16[8,8320]{1,0:T(8,128)(2,1)S(1)} %pad_maximum_fusion.10), channel_id=1, source_target_pairs={{0,2},{2,4},{4,6},{6,8},{8,10},{10,12},{12,14},{14,0},{1,3},{3,5},... | collective-permute-start | bytes 399368 | tf_op jit(solution)/shard_map/ppermute | solution.py:18
  20.2 6.2 %collective-permute-start.1 = (bf16[8,8320]{1,0:T(8,128)(2,1)S(1)}, bf16[8,8320]{1,0:T(8,128)(2,1)S(1)}, u32[]{:S(2)}, u32[]{:S(2)}) collective-permute-start(bf16[8,8320]{1,0:T(8,128)(2,1)S(1)} %collective-permute-done), channel_id=1, source_target_pairs={{0,14},{2,0},{4,2},{6,4},{8,6},{10,8},{12,10},{14,12},{1,15},{3,1}... | collective-permute-start | bytes 399368 | tf_op jit(solution)/shard_map/ppermute | solution.py:18
  23.9 6.2 %collective-permute-start.5 = (bf16[8,8320]{1,0:T(8,128)(2,1)S(1)}, bf16[8,8320]{1,0:T(8,128)(2,1)S(1)}, u32[]{:S(2)}, u32[]{:S(2)}) collective-permute-start(bf16[8,8320]{1,0:T(8,128)(2,1)S(1)} %collective-permute-done.4), channel_id=1, source_target_pairs={{0,2},{2,4},{4,6},{6,8},{8,10},{10,12},{12,14},{14,0},{1,3},{3,5},... | collective-permute-start | bytes 399368 | tf_op jit(solution)/shard_map/ppermute | solution.py:18
  26.5 6.2 %collective-permute-start.2 = (bf16[8,8320]{1,0:T(8,128)(2,1)S(1)}, bf16[8,8320]{1,0:T(8,128)(2,1)S(1)}, u32[]{:S(2)}, u32[]{:S(2)}) collective-permute-start(bf16[8,8320]{1,0:T(8,128)(2,1)S(1)} %collective-permute-done.1), channel_id=1, source_target_pairs={{0,14},{2,0},{4,2},{6,4},{8,6},{10,8},{12,10},{14,12},{1,15},{3,1}... | collective-permute-start | bytes 399368 | tf_op jit(solution)/shard_map/ppermute | solution.py:18
  30.1 6.2 %collective-permute-start.6 = (bf16[8,8320]{1,0:T(8,128)(2,1)S(1)}, bf16[8,8320]{1,0:T(8,128)(2,1)S(1)}, u32[]{:S(2)}, u32[]{:S(2)}) collective-permute-start(bf16[8,8320]{1,0:T(8,128)(2,1)S(1)} %collective-permute-done.5), channel_id=1, source_target_pairs={{0,2},{2,4},{4,6},{6,8},{8,10},{10,12},{12,14},{14,0},{1,3},{3,5},... | collective-permute-start | bytes 399368 | tf_op jit(solution)/shard_map/ppermute | solution.py:18
  32.7 9.3 %collective-permute-start.3 = (bf16[8,4224]{1,0:T(8,128)(2,1)S(1)}, bf16[8,4224]{1,0:T(8,128)(2,1)S(1)}, u32[]{:S(2)}, u32[]{:S(2)}) collective-permute-start(bf16[8,4224]{1,0:T(8,128)(2,1)S(1)} %slice.275), channel_id=1, source_target_pairs={{0,14},{2,0},{4,2},{6,4},{8,6},{10,8},{12,10},{14,12},{1,15},{3,1}... | collective-permute-start | bytes 202760 | tf_op jit(solution)/shard_map/ppermute | solution.py:18
  36.4 5.6 %collective-permute-start.9 = (bf16[8,4096]{1,0:T(8,128)(2,1)S(1)}, bf16[8,4096]{1,0:T(8,128)(2,1)S(1)}, u32[]{:S(2)}, u32[]{:S(2)}) collective-permute-start(bf16[8,4096]{1,0:T(8,128)(2,1)S(1)} %slice.282), channel_id=1, source_target_pairs={{0,2},{2,4},{4,6},{6,8},{8,10},{10,12},{12,14},{14,0},{1,3},{3,5},... | collective-permute-start | bytes 196616 | tf_op jit(solution)/shard_map/ppermute | solution.py:18
  42.1 17.2 %collective-permute-start.7 = (bf16[8,8,4224]{2,1,0:T(8,128)(2,1)S(1)}, bf16[8,8,4224]{2,1,0:T(8,128)(2,1)S(1)}, u32[]{:S(2)}, u32[]{:S(2)}) collective-permute-start(bf16[8,8,4224]{2,1,0:T(8,128)(2,1)S(1)} %fusion.17), channel_id=1, source_target_pairs={{0,48},{16,0},{32,16},{48,32},{1,49},{17,1},{33,17},{49,33},{2,50}... | collective-permute-start | bytes 1622024 | tf_op jit(solution)/shard_map/ppermute | solution.py:18
  42.7 16.5 %collective-permute-start.8 = (bf16[8,8,4224]{2,1,0:T(8,128)(2,1)S(1)}, bf16[8,8,4224]{2,1,0:T(8,128)(2,1)S(1)}, u32[]{:S(2)}, u32[]{:S(2)}) collective-permute-start(bf16[8,8,4224]{2,1,0:T(8,128)(2,1)S(1)} %fusion.17), channel_id=1, source_target_pairs={{0,16},{16,32},{32,48},{48,0},{1,17},{17,33},{33,49},{49,1},{2,18}... | collective-permute-start | bytes 1622024 | tf_op jit(solution)/shard_map/ppermute | solution.py:18
  44.2 11.3 %collective-permute-start.10 = (bf16[8,8,4096]{2,1,0:T(8,128)(2,1)S(1)}, bf16[8,8,4096]{2,1,0:T(8,128)(2,1)S(1)}, u32[]{:S(2)}, u32[]{:S(2)}) collective-permute-start(bf16[8,8,4096]{2,1,0:T(8,128)(2,1)S(1)} %fusion.22), channel_id=1, source_target_pairs={{0,192},{64,0},{128,64},{192,128},{1,193},{65,1},{129,65},{193,129... | collective-permute-start | bytes 1572872 | tf_op jit(solution)/shard_map/ppermute | solution.py:18
  47.2 12.0 %collective-permute-start.11 = (bf16[8,8,4096]{2,1,0:T(8,128)(2,1)S(1)}, bf16[8,8,4096]{2,1,0:T(8,128)(2,1)S(1)}, u32[]{:S(2)}, u32[]{:S(2)}) collective-permute-start(bf16[8,8,4096]{2,1,0:T(8,128)(2,1)S(1)} %fusion.22), channel_id=1, source_target_pairs={{0,64},{64,128},{128,192},{192,0},{1,65},{65,129},{129,193},{193,1... | collective-permute-start | bytes 1572872 | tf_op jit(solution)/shard_map/ppermute | solution.py:18
  59.3 6.4 %collective-permute-start.14 = (bf16[4,8,4096]{2,1,0:T(8,128)(2,1)S(1)}, bf16[4,8,4096]{2,1,0:T(8,128)(2,1)S(1)}, u32[]{:S(2)}, u32[]{:S(2)}) collective-permute-start(bf16[4,8,4096]{2,1,0:T(8,128)(2,1)S(1)} %slice.226), channel_id=1, source_target_pairs={{0,192},{64,0},{128,64},{192,128},{1,193},{65,1},{129,65},{193,129... | collective-permute-start | bytes 786440 | tf_op jit(solution)/shard_map/ppermute | solution.py:18
  59.4 7.7 %collective-permute-start.15 = (bf16[4,8,4096]{2,1,0:T(8,128)(2,1)S(1)}, bf16[4,8,4096]{2,1,0:T(8,128)(2,1)S(1)}, u32[]{:S(2)}, u32[]{:S(2)}) collective-permute-start(bf16[4,8,4096]{2,1,0:T(8,128)(2,1)S(1)} %slice.227), channel_id=1, source_target_pairs={{0,64},{64,128},{128,192},{192,0},{1,65},{65,129},{129,193},{193,1... | collective-permute-start | bytes 786440 | tf_op jit(solution)/shard_map/ppermute | solution.py:18
  61.5 7.8 %collective-permute-start.12 = (bf16[4,8,4224]{2,1,0:T(8,128)(2,1)S(1)}, bf16[4,8,4224]{2,1,0:T(8,128)(2,1)S(1)}, u32[]{:S(2)}, u32[]{:S(2)}) collective-permute-start(bf16[4,8,4224]{2,1,0:T(8,128)(2,1)S(1)} %slice.224), channel_id=1, source_target_pairs={{0,48},{16,0},{32,16},{48,32},{1,49},{17,1},{33,17},{49,33},{2,50}... | collective-permute-start | bytes 811016 | tf_op jit(solution)/shard_map/ppermute | solution.py:18
  62.2 9.1 %collective-permute-start.13 = (bf16[4,8,4224]{2,1,0:T(8,128)(2,1)S(1)}, bf16[4,8,4224]{2,1,0:T(8,128)(2,1)S(1)}, u32[]{:S(2)}, u32[]{:S(2)}) collective-permute-start(bf16[4,8,4224]{2,1,0:T(8,128)(2,1)S(1)} %slice.225), channel_id=1, source_target_pairs={{0,16},{16,32},{32,48},{48,0},{1,17},{17,33},{33,49},{49,1},{2,18}... | collective-permute-start | bytes 811016 | tf_op jit(solution)/shard_map/ppermute | solution.py:18
  67.4 13.1 %copy-start.1 = (bf16[4,8,8,4096]{3,2,1,0:T(8,128)(2,1)}, bf16[4,8,8,4096]{3,2,1,0:T(8,128)(2,1)S(1)}, u32[]{:S(2)}) copy-start(bf16[4,8,8,4096]{3,2,1,0:T(8,128)(2,1)S(1)} %pad_maximum_fusion.4.refs_5_.refs_7_) | copy-start | bytes 6291460
  71.3 1.4 copy-start.8
  71.4 1.9 copy-start.6
  71.4 2.4 copy-start.7
  73.8 3.5 copy-start
  74.3 8.0 %collective-permute-start.20 = (bf16[3,192,4096]{2,1,0:T(8,128)(2,1)S(1)}, bf16[3,192,4096]{2,1,0:T(8,128)(2,1)S(1)}, u32[]{:S(2)}, u32[]{:S(2)}) collective-permute-start(bf16[3,192,4096]{2,1,0:T(8,128)(2,1)S(1)} %pad_maximum_fusion.1), channel_id=1, source_target_pairs={{0,1},{1,0},{2,3},{3,2},{4,5},{5,4},{6,7},{7,6},{8,9},{9,8},{10,11... | collective-permute-start | bytes 14155784 | tf_op jit(solution)/shard_map/ppermute | solution.py:18
  74.4 75.0 %collective-permute-start.16 = (bf16[4,8,8,4224]{3,2,1,0:T(8,128)(2,1)S(1)}, bf16[4,8,8,4224]{3,2,1,0:T(8,128)(2,1)S(1)}, u32[]{:S(2)}, u32[]{:S(2)}) collective-permute-start(bf16[4,8,8,4224]{3,2,1,0:T(8,128)(2,1)S(1)} %pad_maximum_fusion.3.refs_0_.refs_2_), channel_id=1, source_target_pairs={{0,192},{64,0},{128,64},{192,128},{1,193},{65,1},{129,65},{193,129... | collective-permute-start | bytes 6488072 | tf_op jit(solution)/shard_map/ppermute | solution.py:18
  77.3 73.0 %collective-permute-start.17 = (bf16[4,8,8,4224]{3,2,1,0:T(8,128)(2,1)S(1)}, bf16[4,8,8,4224]{3,2,1,0:T(8,128)(2,1)S(1)}, u32[]{:S(2)}, u32[]{:S(2)}) collective-permute-start(bf16[4,8,8,4224]{3,2,1,0:T(8,128)(2,1)S(1)} %pad_maximum_fusion.3.refs_0_.refs_2_), channel_id=1, source_target_pairs={{0,64},{64,128},{128,192},{192,0},{1,65},{65,129},{129,193},{193,1... | collective-permute-start | bytes 6488072 | tf_op jit(solution)/shard_map/ppermute | solution.py:18
  77.3 68.1 %collective-permute-start.18 = (bf16[4,8,8,4096]{3,2,1,0:T(8,128)(2,1)S(1)}, bf16[4,8,8,4096]{3,2,1,0:T(8,128)(2,1)S(1)}, u32[]{:S(2)}, u32[]{:S(2)}) collective-permute-start(bf16[4,8,8,4096]{3,2,1,0:T(8,128)(2,1)S(1)} %pad_maximum_fusion.4.refs_5_.refs_7_), channel_id=1, source_target_pairs={{0,48},{16,0},{32,16},{48,32},{1,49},{17,1},{33,17},{49,33},{2,50}... | collective-permute-start | bytes 6291464 | tf_op jit(solution)/shard_map/ppermute | solution.py:18
  80.5 68.4 %collective-permute-start.19 = (bf16[4,8,8,4096]{3,2,1,0:T(8,128)(2,1)S(1)}, bf16[4,8,8,4096]{3,2,1,0:T(8,128)(2,1)S(1)}, u32[]{:S(2)}, u32[]{:S(2)}) collective-permute-start(bf16[4,8,8,4096]{3,2,1,0:T(8,128)(2,1)S(1)} %pad_maximum_fusion.4.refs_5_.refs_7_), channel_id=1, source_target_pairs={{0,16},{16,32},{32,48},{48,0},{1,17},{17,33},{33,49},{49,1},{2,18}... | collective-permute-start | bytes 6291464 | tf_op jit(solution)/shard_map/ppermute | solution.py:18
  145.4 10.0 %copy-start.4 = (bf16[4,8,8,4096]{3,2,1,0:T(8,128)(2,1)}, bf16[4,8,8,4096]{3,2,1,0:T(8,128)(2,1)S(1)}, u32[]{:S(2)}) copy-start(bf16[4,8,8,4096]{3,2,1,0:T(8,128)(2,1)S(1)} %collective-permute-done.18.refs_6_.refs_8_) | copy-start | bytes 6291460
  148.8 10.2 %copy-start.5 = (bf16[4,8,8,4096]{3,2,1,0:T(8,128)(2,1)}, bf16[4,8,8,4096]{3,2,1,0:T(8,128)(2,1)S(1)}, u32[]{:S(2)}) copy-start(bf16[4,8,8,4096]{3,2,1,0:T(8,128)(2,1)S(1)} %collective-permute-done.19.refs_9_.refs_11_) | copy-start | bytes 6291460
  149.4 5.9 %copy-start.2 = (bf16[4,8,8,4224]{3,2,1,0:T(8,128)(2,1)}, bf16[4,8,8,4224]{3,2,1,0:T(8,128)(2,1)S(1)}, u32[]{:S(2)}) copy-start(bf16[4,8,8,4224]{3,2,1,0:T(8,128)(2,1)S(1)} %collective-permute-done.16.refs_1_.refs_3_) | copy-start | bytes 6488068
  150.3 5.1 %copy-start.3 = (bf16[4,8,8,4224]{3,2,1,0:T(8,128)(2,1)}, bf16[4,8,8,4224]{3,2,1,0:T(8,128)(2,1)S(1)}, u32[]{:S(2)}) copy-start(bf16[4,8,8,4224]{3,2,1,0:T(8,128)(2,1)S(1)} %collective-permute-done.17.refs_4_.refs_6_) | copy-start | bytes 6488068
  151.4 46.3 %collective-permute-start.21 = (bf16[2,8,8,4224]{3,2,1,0:T(8,128)(2,1)}, bf16[2,8,8,4224]{3,2,1,0:T(8,128)(2,1)S(1)}, u32[]{:S(2)}, u32[]{:S(2)}) collective-permute-start(bf16[2,8,8,4224]{3,2,1,0:T(8,128)(2,1)} %slice.231), channel_id=1, source_target_pairs={{0,192},{64,0},{128,64},{192,128},{1,193},{65,1},{129,65},{193,129... | collective-permute-start | bytes 3244040 | tf_op jit(solution)/shard_map/ppermute | solution.py:18
  155.4 44.2 %collective-permute-start.22 = (bf16[2,8,8,4224]{3,2,1,0:T(8,128)(2,1)}, bf16[2,8,8,4224]{3,2,1,0:T(8,128)(2,1)S(1)}, u32[]{:S(2)}, u32[]{:S(2)}) collective-permute-start(bf16[2,8,8,4224]{3,2,1,0:T(8,128)(2,1)} %slice.232), channel_id=1, source_target_pairs={{0,64},{64,128},{128,192},{192,0},{1,65},{65,129},{129,193},{193,1... | collective-permute-start | bytes 3244040 | tf_op jit(solution)/shard_map/ppermute | solution.py:18
  156.4 39.1 %collective-permute-start.23 = (bf16[2,8,8,4096]{3,2,1,0:T(8,128)(2,1)}, bf16[2,8,8,4096]{3,2,1,0:T(8,128)(2,1)S(1)}, u32[]{:S(2)}, u32[]{:S(2)}) collective-permute-start(bf16[2,8,8,4096]{3,2,1,0:T(8,128)(2,1)} %slice.233), channel_id=1, source_target_pairs={{0,48},{16,0},{32,16},{48,32},{1,49},{17,1},{33,17},{49,33},{2,50}... | collective-permute-start | bytes 3145736 | tf_op jit(solution)/shard_map/ppermute | solution.py:18
  160.1 36.7 %collective-permute-start.24 = (bf16[2,8,8,4096]{3,2,1,0:T(8,128)(2,1)}, bf16[2,8,8,4096]{3,2,1,0:T(8,128)(2,1)}, u32[]{:S(2)}, u32[]{:S(2)}) collective-permute-start(bf16[2,8,8,4096]{3,2,1,0:T(8,128)(2,1)} %slice.234), channel_id=1, source_target_pairs={{0,16},{16,32},{32,48},{48,0},{1,17},{17,33},{33,49},{49,1},{2,18}... | collective-permute-start | bytes 3145736 | tf_op jit(solution)/shard_map/ppermute | solution.py:18
  195.5 4.0 copy-start.11
  197.7 1.9 copy-start.9
  199.5 1.0 copy-start.10
  236.5 25.2 %collective-permute-start.25 = (bf16[2,8,8,4096]{3,2,1,0:T(8,128)(2,1)}, bf16[2,8,8,4096]{3,2,1,0:T(8,128)(2,1)S(1)}, u32[]{:S(2)}, u32[]{:S(2)}) collective-permute-start(bf16[2,8,8,4096]{3,2,1,0:T(8,128)(2,1)} %get-tuple-element.99), channel_id=1, source_target_pairs={{0,16},{16,32},{32,48},{48,0},{1,17},{17,33},{33,49},{49,1},{2,18}... | collective-permute-start | bytes 3145736 | tf_op jit(solution)/shard_map/ppermute | solution.py:18
  237.6 24.8 %collective-permute-start.26 = (bf16[2,8,8,4096]{3,2,1,0:T(8,128)(2,1)}, bf16[2,8,8,4096]{3,2,1,0:T(8,128)(2,1)}, u32[]{:S(2)}, u32[]{:S(2)}) collective-permute-start(bf16[2,8,8,4096]{3,2,1,0:T(8,128)(2,1)} %get-tuple-element.98), channel_id=1, source_target_pairs={{0,48},{16,0},{32,16},{48,32},{1,49},{17,1},{33,17},{49,33},{2,50}... | collective-permute-start | bytes 3145736 | tf_op jit(solution)/shard_map/ppermute | solution.py:18
  265.4 28.2 %collective-permute-start.27 = (bf16[2,8,8,4096]{3,2,1,0:T(8,128)(2,1)}, bf16[2,8,8,4096]{3,2,1,0:T(8,128)(2,1)}, u32[]{:S(2)}, u32[]{:S(2)}) collective-permute-start(bf16[2,8,8,4096]{3,2,1,0:T(8,128)(2,1)} %get-tuple-element.121), channel_id=1, source_target_pairs={{0,64},{64,128},{128,192},{192,0},{1,65},{65,129},{129,193},{193,1... | collective-permute-start | bytes 3145736 | tf_op jit(solution)/shard_map/ppermute | solution.py:18
  265.6 28.0 %collective-permute-start.28 = (bf16[2,8,8,4096]{3,2,1,0:T(8,128)(2,1)}, bf16[2,8,8,4096]{3,2,1,0:T(8,128)(2,1)}, u32[]{:S(2)}, u32[]{:S(2)}) collective-permute-start(bf16[2,8,8,4096]{3,2,1,0:T(8,128)(2,1)} %get-tuple-element.120), channel_id=1, source_target_pairs={{0,192},{64,0},{128,64},{192,128},{1,193},{65,1},{129,65},{193,129... | collective-permute-start | bytes 3145736 | tf_op jit(solution)/shard_map/ppermute | solution.py:18
  290.9 52.5 %collective-permute-start.36 = (bf16[4,8,8,4096]{3,2,1,0:T(8,128)(2,1)S(1)}, bf16[4,8,8,4096]{3,2,1,0:T(8,128)(2,1)}, u32[]{:S(2)}, u32[]{:S(2)}) collective-permute-start(bf16[4,8,8,4096]{3,2,1,0:T(8,128)(2,1)S(1)} %pad_maximum_fusion.8), channel_id=1, source_target_pairs={{0,48},{16,0},{32,16},{48,32},{1,49},{17,1},{33,17},{49,33},{2,50}... | collective-permute-start | bytes 6291464 | tf_op jit(solution)/shard_map/ppermute | solution.py:18
  293.3 2.2 copy-start.12
  293.5 49.9 %collective-permute-start.35 = (bf16[4,8,8,4096]{3,2,1,0:T(8,128)(2,1)S(1)}, bf16[4,8,8,4096]{3,2,1,0:T(8,128)(2,1)S(1)}, u32[]{:S(2)}, u32[]{:S(2)}) collective-permute-start(bf16[4,8,8,4096]{3,2,1,0:T(8,128)(2,1)S(1)} %pad_maximum_fusion.7), channel_id=1, source_target_pairs={{0,16},{16,32},{32,48},{48,0},{1,17},{17,33},{33,49},{49,1},{2,18}... | collective-permute-start | bytes 6291464 | tf_op jit(solution)/shard_map/ppermute | solution.py:18
  299.6 73.4 %collective-permute-start.30 = (bf16[4,8,8,4096]{3,2,1,0:T(8,128)(2,1)}, bf16[4,8,8,4096]{3,2,1,0:T(8,128)(2,1)}, u32[]{:S(2)}, u32[]{:S(2)}) collective-permute-start(bf16[4,8,8,4096]{3,2,1,0:T(8,128)(2,1)} %pad_maximum_fusion.6), channel_id=1, source_target_pairs={{0,192},{64,0},{128,64},{192,128},{1,193},{65,1},{129,65},{193,129... | collective-permute-start | bytes 6291464 | tf_op jit(solution)/shard_map/ppermute | solution.py:18
  302.1 70.9 %collective-permute-start.29 = (bf16[4,8,8,4096]{3,2,1,0:T(8,128)(2,1)}, bf16[4,8,8,4096]{3,2,1,0:T(8,128)(2,1)}, u32[]{:S(2)}, u32[]{:S(2)}) collective-permute-start(bf16[4,8,8,4096]{3,2,1,0:T(8,128)(2,1)} %pad_maximum_fusion.5), channel_id=1, source_target_pairs={{0,64},{64,128},{128,192},{192,0},{1,65},{65,129},{129,193},{193,1... | collective-permute-start | bytes 6291464 | tf_op jit(solution)/shard_map/ppermute | solution.py:18
  347.4 10.7 %collective-permute-start.39 = (bf16[4,8,4096]{2,1,0:T(8,128)(2,1)S(1)}, bf16[4,8,4096]{2,1,0:T(8,128)(2,1)S(1)}, u32[]{:S(2)}, u32[]{:S(2)}) collective-permute-start(bf16[4,8,4096]{2,1,0:T(8,128)(2,1)S(1)} %get-tuple-element.116), channel_id=1, source_target_pairs={{0,128},{64,192},{128,0},{192,64},{1,129},{65,193},{129,1},{193,65... | collective-permute-start | bytes 786440 | tf_op jit(solution)/shard_map/ppermute | solution.py:18
  349.0 22.7 %collective-permute-start.37 = (bf16[8,8,4096]{2,1,0:T(8,128)(2,1)}, bf16[8,8,4096]{2,1,0:T(8,128)(2,1)S(1)}, u32[]{:S(2)}, u32[]{:S(2)}) collective-permute-start(bf16[8,8,4096]{2,1,0:T(8,128)(2,1)} %get-tuple-element.118), channel_id=1, source_target_pairs={{0,64},{64,128},{128,192},{192,0},{1,65},{65,129},{129,193},{193,1... | collective-permute-start | bytes 1572872 | tf_op jit(solution)/shard_map/ppermute | solution.py:18
  351.5 20.3 %collective-permute-start.38 = (bf16[8,8,4096]{2,1,0:T(8,128)(2,1)}, bf16[8,8,4096]{2,1,0:T(8,128)(2,1)S(1)}, u32[]{:S(2)}, u32[]{:S(2)}) collective-permute-start(bf16[8,8,4096]{2,1,0:T(8,128)(2,1)} %get-tuple-element.119), channel_id=1, source_target_pairs={{0,192},{64,0},{128,64},{192,128},{1,193},{65,1},{129,65},{193,129... | collective-permute-start | bytes 1572872 | tf_op jit(solution)/shard_map/ppermute | solution.py:18
  358.2 13.6 %collective-permute-start.40 = (bf16[4,8,4096]{2,1,0:T(8,128)(2,1)}, bf16[4,8,4096]{2,1,0:T(8,128)(2,1)}, u32[]{:S(2)}, u32[]{:S(2)}) collective-permute-start(bf16[4,8,4096]{2,1,0:T(8,128)(2,1)} %get-tuple-element.117), channel_id=1, source_target_pairs={{0,128},{64,192},{128,0},{192,64},{1,129},{65,193},{129,1},{193,65... | collective-permute-start | bytes 786440 | tf_op jit(solution)/shard_map/ppermute | solution.py:18
  358.8 14.3 %copy-start.13 = (bf16[1,4,8,8,4096]{4,3,2,1,0:T(8,128)(2,1)S(1)}, bf16[1,4,8,8,4096]{4,3,2,1,0:T(8,128)(2,1)}, u32[]{:S(2)}) copy-start(bf16[1,4,8,8,4096]{4,3,2,1,0:T(8,128)(2,1)} %get-tuple-element.76) | copy-start | bytes 6291460
  371.8 34.7 %collective-permute-start.41 = (bf16[3,192,4096]{2,1,0:T(8,128)(2,1)}, bf16[3,192,4096]{2,1,0:T(8,128)(2,1)}, u32[]{:S(2)}, u32[]{:S(2)}) collective-permute-start(bf16[3,192,4096]{2,1,0:T(8,128)(2,1)} %get-tuple-element.95), channel_id=1, source_target_pairs={{0,1},{1,0},{2,3},{3,2},{4,5},{5,4},{6,7},{7,6},{8,9},{9,8},{10,11... | collective-permute-start | bytes 14155784 | tf_op jit(solution)/shard_map/ppermute | solution.py:18
  376.4 28.7 %collective-permute-start.31 = (bf16[8,8,4096]{2,1,0:T(8,128)(2,1)S(1)}, bf16[8,8,4096]{2,1,0:T(8,128)(2,1)S(1)}, u32[]{:S(2)}, u32[]{:S(2)}) collective-permute-start(bf16[8,8,4096]{2,1,0:T(8,128)(2,1)S(1)} %get-tuple-element.114), channel_id=1, source_target_pairs={{0,16},{16,32},{32,48},{48,0},{1,17},{17,33},{33,49},{49,1},{2,18}... | collective-permute-start | bytes 1572872 | tf_op jit(solution)/shard_map/ppermute | solution.py:18
  376.7 28.3 %collective-permute-start.32 = (bf16[8,8,4096]{2,1,0:T(8,128)(2,1)S(1)}, bf16[8,8,4096]{2,1,0:T(8,128)(2,1)S(1)}, u32[]{:S(2)}, u32[]{:S(2)}) collective-permute-start(bf16[8,8,4096]{2,1,0:T(8,128)(2,1)S(1)} %get-tuple-element.115), channel_id=1, source_target_pairs={{0,48},{16,0},{32,16},{48,32},{1,49},{17,1},{33,17},{49,33},{2,50}... | collective-permute-start | bytes 1572872 | tf_op jit(solution)/shard_map/ppermute | solution.py:18
  379.6 20.2 %collective-permute-start.33 = (bf16[4,8,4096]{2,1,0:T(8,128)(2,1)S(1)}, bf16[4,8,4096]{2,1,0:T(8,128)(2,1)S(1)}, u32[]{:S(2)}, u32[]{:S(2)}) collective-permute-start(bf16[4,8,4096]{2,1,0:T(8,128)(2,1)S(1)} %get-tuple-element.112), channel_id=1, source_target_pairs={{0,32},{16,48},{32,0},{48,16},{1,33},{17,49},{33,1},{49,17},{2,34}... | collective-permute-start | bytes 786440 | tf_op jit(solution)/shard_map/ppermute | solution.py:18
  381.7 23.4 %collective-permute-start.34 = (bf16[4,8,4096]{2,1,0:T(8,128)(2,1)S(1)}, bf16[4,8,4096]{2,1,0:T(8,128)(2,1)S(1)}, u32[]{:S(2)}, u32[]{:S(2)}) collective-permute-start(bf16[4,8,4096]{2,1,0:T(8,128)(2,1)S(1)} %get-tuple-element.113), channel_id=1, source_target_pairs={{0,32},{16,48},{32,0},{48,16},{1,33},{17,49},{33,1},{49,17},{2,34}... | collective-permute-start | bytes 786440 | tf_op jit(solution)/shard_map/ppermute | solution.py:18
Sparse Core Ops, SparseCore 0:
  11.9 198.4 all-gather.1
  406.6 36.6 reduce-scatter.1

commit v2 on v1

--- a/solution.py
+++ b/solution.py
@@ -41,15 +41,21 @@
     return near, back
 
 
-def direct_sum(blocks, axis):
+def direct_moves(blocks, axis, whole=False):
     size, far = len(blocks), len(blocks) // 2
+    moved = [shift(b, axis, k if k < far else k - size) for k, b in enumerate(blocks) if k not in (0, far)]
+    if whole:
+        return moved + [shift(blocks[far], axis, far)]
     half = blocks[far].shape[0] // 2
-    moved = [shift(b, axis, k if k < far else k - size) for k, b in enumerate(blocks) if k not in (0, far)]
-    up, down = shift(blocks[far][:half], axis, far), shift(blocks[far][half:], axis, -far)
-    total = blocks[0].astype(F32)
+    return moved, (shift(blocks[far][:half], axis, far), shift(blocks[far][half:], axis, -far))
+
+
+def direct_total(own, moves):
+    moved, halves = moves
+    total = own.astype(F32)
     for block in moved:
         total = total + block.astype(F32)
-    return (total + jnp.concatenate([up, down], axis=0).astype(F32)).astype(BF16)
+    return (total + jnp.concatenate(halves, axis=0).astype(F32)).astype(BF16)
 
 
 def ring_gather4(first, first_axis, second, second_axis, beside=()):
@@ -341,13 +347,14 @@
     rows, dgu1 = lax.optimization_barrier((rows, dgu1))
     first = functools.partial(first_call, ids, wgu=wgu, wd=wd, lanes=lanes)
     p_far, dgu_far, h_far = first(rows, start=2, stop=3, stride=1)
-    ends1, p_far, rows = lax.optimization_barrier((ends1, p_far, rows))
     ends0 = ring_ends4(p_far[0], "x")
-    last1 = ring_ends(*ring_middle4(p1[1], p1[3], ends1), "y")
+    rows, dgu_far = lax.optimization_barrier((rows, dgu_far))
     p_side, dgu_side, h_side = first(rows, start=1, stop=4, stride=2)
-    ends0, p_side, rows = lax.optimization_barrier((ends0, p_side, rows))
+    ends0, ends1, p_side, rows = lax.optimization_barrier((ends0, ends1, p_side, rows))
     near0, back0 = ring_middle4(p_side[0], p_side[1], ends0)
     last0 = ring_ends(near0, back0, "x")
+    ends1, _ = lax.optimization_barrier((ends1, near0))
+    last1 = ring_ends(*ring_middle4(p1[1], p1[3], ends1), "y")
     near0, rows = lax.optimization_barrier((near0, rows))
     p_own, dgu_own, h_own = first(rows, start=0, stop=1, stride=1)
     mine, other = weight_call(
@@ -355,14 +362,23 @@
     )
     last1, other = lax.optimization_barrier((last1, other))
     last0, mine = lax.optimization_barrier((last0, mine))
+    q1 = add(p1[0], *last1)
+    moves1 = direct_moves([q1[k] for k in range(nx)], "x")
+    q0 = add(p_own[0], *last0)
+    moves1, _ = lax.optimization_barrier((moves1, q0))
+    turned = lambda value, start, size: [
+        lax.dynamic_index_in_dim(value, lax.rem(start + k, size), 0, keepdims=False) for k in range(size)
+    ]
+    blocks0 = turned(q0, iy, ny)
+    moves0 = direct_moves(blocks0, "y")
+    r1 = direct_total(q1[0], moves1)
+    r1 = lax.dynamic_slice_in_dim(jnp.concatenate([r1, r1], axis=0), nz - iz, nz, axis=0)
+    s1 = lax.psum_scatter(r1.reshape(nz * half, width), "z", scatter_dimension=0, tiled=True)
     grads = (mine + shift(other, "c", 1).astype(F32)).astype(BF16)
-    q1 = add(p1[0], *last1)
-    r1 = direct_sum([q1[k] for k in range(nx)], "x")
-    r1 = lax.dynamic_slice_in_dim(jnp.concatenate([r1, r1], axis=0), nz - iz, nz, axis=0)
-    q0 = add(p_own[0], *last0)
-    r0 = direct_sum([lax.dynamic_index_in_dim(q0, lax.rem(iy + k, ny), 0, keepdims=False) for k in range(ny)], "y")
-    both = jnp.concatenate([r0, r1], axis=1).reshape(nz * per, width)
-    grad_tokens = lax.psum_scatter(both, "z", scatter_dimension=0, tiled=True)
+    moves0, grads = lax.optimization_barrier((moves0, grads))
+    blocks0 = turned(direct_total(blocks0[0], moves0), iz, nz)
+    s0 = add(blocks0[0], *direct_moves(blocks0, "z", whole=True))
+    grad_tokens = jnp.concatenate([s0, s1], axis=0)
     return grad_tokens, grads[0:1], grads[1:2], grads[2:3]
 
 

time: 460 us -> 457 us (level)
  waiting for transfers between devices: 206 us -> 180 us
  starting transfers between devices: 60.1 us -> 78.9 us
    ppermute x42 -> x49, starting transfers between devices: 60 us -> 78.8 us  [shift(): lax.ppermute(value, axis, [(i, (i + by) % size) for i in range(size)])]
    ppermute x42 -> x49, waiting for transfers between devices: 178 us -> 162 us  [shift(): lax.ppermute(value, axis, [(i, (i + by) % size) for i in range(size)])]
    reduce_scatter x1, waiting for transfers between devices: 27.9 us -> 17.9 us  [on_device(): lax.psum_scatter(r1.reshape(nz * half, width), 'z', scatter_dimension=0,...]
    convert_element_type x4 -> x5, other arithmetic: 11.5 us -> 10.9 us  [add(): return total.astype(BF16)]
  transfers between devices with their start and end apart: 44 -> 51, of which waited for: 26 -> 29; matrix products, arithmetic and copies ran while one was open for 12% -> 12% of each run, Pallas kernels for 23% -> 23%
where the time goes in v2:
time: 457 us; the launch traced here: 448 us
  waiting for transfers between devices  180 us (39%)
  Pallas kernels  104 us (23%)
  starting transfers between devices  78.9 us (17%)
  other arithmetic  42.3 us (9%)
  local copies, waits for them, and re-layouts  28.2 us (6%)
  between operations  15 us (3%)
    ppermute x49, waiting for transfers between devices, shift(): lax.ppermute(value, axis, [(i, (i + by) % size) for i in range(size)])  162 us
    ppermute x49, starting transfers between devices, shift(): lax.ppermute(value, axis, [(i, (i + by) % size) for i in range(size)])  78.8 us
    pallas_call x3, Pallas kernels, first_call(): pl.pallas_call(first_kernel, grid_spec=pltpu.PrefetchScalarGridSpec(num_s...  44.8 us
    pallas_call x1, Pallas kernels, second_call(): pl.pallas_call(second_kernel, grid_spec=pltpu.PrefetchScalarGridSpec(num_...  31.9 us
    pallas_call x1, Pallas kernels, weight_call(): pl.pallas_call(weight_kernel, grid_spec=pltpu.PrefetchScalarGridSpec(num_...  27.3 us
    reduce_scatter x1, waiting for transfers between devices, on_device(): lax.psum_scatter(r1.reshape(nz * half, width), 'z', scatter_dimension=0,...  17.9 us
    concatenate x1, other arithmetic, on_device(): wgu = jnp.concatenate([w_gate[0], swapped[0], w_up[0], swapped[1]], axis=0)  11.2 us
    convert_element_type x5, other arithmetic, add(): return total.astype(BF16)  10.9 us
  transfers between devices with their start and end apart: 51, of which 29 were waited for; matrix products, arithmetic and copies ran while one was open for 12% of the time, Pallas kernels for 23%

profile of v2, /device:TPU:8, one launch (start us, length us, event | category | flops | bytes accessed | tf_op | source)
XLA Modules:
  0.0 448.4 jit_solution(12913572820175049373)
XLA Ops:
  11.5 5.9 %collective-permute-start = (bf16[8,8320]{1,0:T(8,128)(2,1)S(1)}, bf16[8,8320]{1,0:T(8,128)(2,1)S(1)}, u32[]{:S(2)}, u32[]{:S(2)}) collective-permute-start(bf16[8,8320]{1,0:T(8,128)(2,1)S(1)} %pad_maximum_fusion.9), channel_id=1, source_target_pairs={{0,14},{2,0},{4,2},{6,4},{8,6},{10,8},{12,10},{14,12},{1,15},{3,1}... | collective-permute-start | bytes 399368 | tf_op jit(solution)/shard_map/ppermute | solution.py:18
  18.3 1.9 collective-permute-done
  20.3 3.7 collective-permute-start.1
  24.0 2.5 collective-permute-done.1
  26.5 3.7 collective-permute-start.2
  30.2 2.5 collective-permute-done.2
  32.7 3.7 collective-permute-start.3
  36.5 5.5 %collective-permute-done.9 = bf16[8,4096]{1,0:T(8,128)(2,1)S(1)} collective-permute-done((bf16[8,4096]{1,0:T(8,128)(2,1)S(1)}, bf16[8,4096]{1,0:T(8,128)(2,1)S(1)}, u32[]{:S(2)}, u32[]{:S(2)}) %collective-permute-start.9) | collective-permute-done | bytes 65568 | tf_op jit(solution)/shard_map/ppermute | solution.py:18
  42.7 1.5 collective-permute-start.8
  44.2 3.0 collective-permute-start.10
  47.2 8.2 %collective-permute-done.10 = bf16[8,8,4096]{2,1,0:T(8,128)(2,1)S(1)} collective-permute-done((bf16[8,8,4096]{2,1,0:T(8,128)(2,1)S(1)}, bf16[8,8,4096]{2,1,0:T(8,128)(2,1)S(1)}, u32[]{:S(2)}, u32[]{:S(2)}) %collective-permute-start.10) | collective-permute-done | bytes 524320 | tf_op jit(solution)/shard_map/ppermute | solution.py:18
  55.5 3.8 collective-permute-done.11
  59.4 2.1 collective-permute-start.15
  62.2 1.7 collective-permute-start.13
  63.9 1.8 collective-permute-done.14
  67.4 2.0 collective-permute-done.12
  69.4 1.9 collective-permute-done.13
  74.4 2.9 collective-permute-start.16
  77.3 3.2 collective-permute-start.18
  80.5 1.9 collective-permute-done.20
  82.8 1.9 pad_maximum_fusion.2.refs_11_.wd_ref
  84.7 11.2 %pad_maximum_fusion.refs_10_.wgu_ref = bf16[768,4096]{1,0:T(8,128)(2,1)} fusion(bf16[192,4096]{1,0:T(8,128)(2,1)S(1)} %get-tuple-element.128, bf16[192,4096]{1,0:T(8,128)(2,1)S(1)} %bitcast.167, bf16[192,4096]{1,0:T(8,128)(2,1)S(1)} %get-tuple-element.129, bf16[192,4096]{1,0:T(8,128)(2,1)S(1)} %bitcast.168), kind=kLoop, calls=%fused_computation.1 | loop fusion | flops 25165824 | bytes 12582912 | tf_op jit(solution)/shard_map/concatenate | solution.py:341
  95.8 49.4 %collective-permute-done.18.refs_6_.refs_8_ = bf16[4,8,8,4096]{3,2,1,0:T(8,128)(2,1)S(1)} collective-permute-done((bf16[4,8,8,4096]{3,2,1,0:T(8,128)(2,1)S(1)}, bf16[4,8,8,4096]{3,2,1,0:T(8,128)(2,1)S(1)}, u32[]{:S(2)}, u32[]{:S(2)}) %collective-permute-start.18) | collective-permute-done | bytes 2097184 | tf_op jit(solution)/shard_map/ppermute | solution.py:18
  145.3 3.4 collective-permute-done.19.refs_9_.refs_11_
  151.2 2.9 collective-permute-start.21
  156.2 2.7 collective-permute-start.23
  161.0 34.5 %collective-permute-done.23.refs_7_.refs_9_ = bf16[2,8,8,4096]{3,2,1,0:T(8,128)(2,1)S(1)} collective-permute-done((bf16[2,8,8,4096]{3,2,1,0:T(8,128)(2,1)}, bf16[2,8,8,4096]{3,2,1,0:T(8,128)(2,1)S(1)}, u32[]{:S(2)}, u32[]{:S(2)}) %collective-permute-start.23) | collective-permute-done | bytes 1048608 | tf_op jit(solution)/shard_map/ppermute | solution.py:18
  197.7 1.9 collective-permute-done.22.refs_3_.refs_5_
  200.5 31.9 %tokens_second.1 = (bf16[4,4,8,8,4096]{4,3,2,1,0:T(8,128)(2,1)}, bf16[4,768,256]{2,1,0:T(8,128)(2,1)}, bf16[4,384,256]{2,1,0:T(8,128)(2,1)}) custom-call(s32[5]{0:T(128)} %stack.107.ids, bf16[4,8,8,4224]{3,2,1,0:T(8,128)(2,1)} %copy-done, bf16[4,8,8,4224]{3,2,1,0:T(8,128)(2,1)} %copy-done.2, bf16[2,8,8,4224]{3,2,1,0:T(8,128)(2,1)} %copy-done.10, ...), custom_call_target="tpu_custom_call" | custom-call | tf_op jit(solution)/shard_map/tokens_second/pallas_call | solution.py:203
  232.4 3.9 slice_bitcast_fusion.3
  238.4 12.7 %tokens_first2.1 = (bf16[1,4,8,8,4096]{4,3,2,1,0:T(8,128)(2,1)}, bf16[1,768,256]{2,1,0:T(8,128)(2,1)}, bf16[1,384,256]{2,1,0:T(8,128)(2,1)}) custom-call(s32[5]{0:T(128)} %stack.107.ids, bf16[4,4,8,2,2,8,4224]{6,5,4,3,2,1,0:T(8,128)(2,1)} %bitcast.154, bf16[4,4,8,2,2,8,4224]{6,5,4,3,2,1,0:T(8,128)(2,1)} %bitcast.155, ...), custom_call_target="tpu_custom_call" | custom-call | tf_op jit(solution)/shard_map/tokens_first2/pallas_call | solution.py:127
  251.1 1.7 slice_bitcast_fusion.9
  253.8 2.6 collective-permute-start.26
  256.3 19.2 %tokens_first1.1 = (bf16[2,4,8,8,4096]{4,3,2,1,0:T(8,128)(2,1)}, bf16[2,768,256]{2,1,0:T(8,128)(2,1)}, bf16[2,384,256]{2,1,0:T(8,128)(2,1)}) custom-call(s32[5]{0:T(128)} %stack.107.ids, bf16[4,4,8,2,2,8,4224]{6,5,4,3,2,1,0:T(8,128)(2,1)} %bitcast.157, bf16[4,4,8,2,2,8,4224]{6,5,4,3,2,1,0:T(8,128)(2,1)} %bitcast.158, ...), custom_call_target="tpu_custom_call" | custom-call | tf_op jit(solution)/shard_map/tokens_first1/pallas_call | solution.py:127
  275.6 3.0 collective-permute-done.25
  278.6 1.9 slice_bitcast_fusion.5
  282.1 1.5 pad_maximum_fusion.6
  283.6 3.1 collective-permute-start.30
  286.7 1.5 pad_maximum_fusion.5
  288.2 2.7 fusion.4
  290.9 1.5 pad_maximum_fusion.8
  292.4 3.0 collective-permute-start.36
  296.0 12.8 %tokens_first0.1 = (bf16[1,4,8,8,4096]{4,3,2,1,0:T(8,128)(2,1)}, bf16[1,768,256]{2,1,0:T(8,128)(2,1)}, bf16[1,384,256]{2,1,0:T(8,128)(2,1)}) custom-call(s32[5]{0:T(128)} %stack.107.ids, bf16[4,4,8,2,2,8,4224]{6,5,4,3,2,1,0:T(8,128)(2,1)} %bitcast.160, bf16[4,4,8,2,2,8,4224]{6,5,4,3,2,1,0:T(8,128)(2,1)} %bitcast.161, ...), custom_call_target="tpu_custom_call" | custom-call | tf_op jit(solution)/shard_map/tokens_first0/pallas_call | solution.py:127
  308.8 27.3 %weights.1 = (f32[3,192,4096]{2,1,0:T(8,128)}, bf16[3,192,4096]{2,1,0:T(8,128)(2,1)}) custom-call(s32[5]{0:T(128)} %stack.107.ids, bf16[4,4,8,2,2,8,4224]{6,5,4,3,2,1,0:T(8,128)(2,1)} %bitcast.163, bf16[4,4,8,2,2,8,4224]{6,5,4,3,2,1,0:T(8,128)(2,1)} %bitcast.164, bf16[4,8,8,4224]{3,2,1,0:T(8,128)(2,1)} %copy-done, bf16[4,8,8,4224]{3,2,1,0:T(8,128)(2,1)} %copy-done.2, ...), custom_call_target="tpu_custom_call" | custom-call | tf_op jit(solution)/shard_map/weights/pallas_call | solution.py:285
  336.1 2.4 collective-permute-done.36
  338.5 2.5 collective-permute-done.35
  340.9 4.1 fusion.1
  345.2 3.2 collective-permute-start.46
  349.7 2.3 collective-permute-start.48
  352.1 3.3 fusion.3
  357.4 10.6 %collective-permute-done.47 = bf16[4,8,4096]{2,1,0:T(8,128)(2,1)S(1)} collective-permute-done((bf16[4,8,4096]{2,1,0:T(8,128)(2,1)S(1)}, bf16[4,8,4096]{2,1,0:T(8,128)(2,1)S(1)}, u32[]{:S(2)}, u32[]{:S(2)}) %collective-permute-start.47) | collective-permute-done | bytes 262176 | tf_op jit(solution)/shard_map/ppermute | solution.py:18
  368.2 4.9 %collective-permute-done.48 = bf16[4,8,4096]{2,1,0:T(8,128)(2,1)S(1)} collective-permute-done((bf16[4,8,4096]{2,1,0:T(8,128)(2,1)S(1)}, bf16[4,8,4096]{2,1,0:T(8,128)(2,1)S(1)}, u32[]{:S(2)}, u32[]{:S(2)}) %collective-permute-start.48) | collective-permute-done | bytes 262176 | tf_op jit(solution)/shard_map/ppermute | solution.py:18
  373.2 2.0 collective-permute-start.32
  375.1 3.5 collective-permute-start.34
  379.8 6.3 %add_convert_fusion = bf16[3,192,4096]{2,1,0:T(8,128)(2,1)} fusion(f32[3,192,4096]{2,1,0:T(8,128)S(1)} %bitcast.166, bf16[3,192,4096]{2,1,0:T(8,128)(2,1)} %collective-permute-done.37), kind=kLoop, calls=%fused_computation | loop fusion | flops 7077888 | bytes 18874368 | tf_op jit(solution)/shard_map/convert_element_type | solution.py:377
  386.1 7.9 %collective-permute-done.33 = bf16[4,8,4096]{2,1,0:T(8,128)(2,1)} collective-permute-done((bf16[4,8,4096]{2,1,0:T(8,128)(2,1)}, bf16[4,8,4096]{2,1,0:T(8,128)(2,1)}, u32[]{:S(2)}, u32[]{:S(2)}) %collective-permute-start.33) | collective-permute-done | bytes 262176 | tf_op jit(solution)/shard_map/ppermute | solution.py:18
  394.0 4.3 collective-permute-done.34
  398.5 1.8 fusion.13
  402.2 4.1 collective-permute-start.40
  407.3 4.1 collective-permute-start.42
  412.7 4.2 collective-permute-start.44
  416.9 4.7 %fusion.36 = (bf16[1,192,4096]{2,1,0:T(8,128)(2,1)}, bf16[1,192,4096]{2,1,0:T(8,128)(2,1)}, bf16[1,192,4096]{2,1,0:T(8,128)(2,1)}) fusion(bf16[3,192,4096]{2,1,0:T(8,128)(2,1)} %add_convert_fusion), kind=kLoop, calls=%fused_computation.109 | loop fusion | bytes 9437184 | tf_op jit(solution)/shard_map/slice | solution.py:382
  421.7 17.9 %reduce-scatter.2.cloned.1.call-done = bf16[8,4096]{1,0:T(8,128)(2,1)} async-done(((bf16[64,4096]{1,0:T(8,128)(2,1)}), bf16[8,4096]{1,0:T(8,128)(2,1)}) %reduce-scatter.2.cloned.1.call-update) | async-done | bytes 65552 | tf_op jit(solution)/shard_map/reduce_scatter | solution.py:376
  439.6 1.5 pad_maximum_fusion.10
  (151 shorter events, 36.3 us)
Async XLA Ops:
  7.2 231.2 %all-gather.2.cloned.1.call-start = ((), (), s32[]{:S(2)}) async-start(), calls=%async_computation.1 | async-start | bytes 34738176 | tf_op jit(solution)/shard_map/all_gather | solution.py:331
  11.5 428.1 %reduce-scatter.2.cloned.1.call-start = ((), (), s32[]{:S(2)}) async-start(), calls=%async_computation.2 | async-start | bytes 589824 | tf_op jit(solution)/shard_map/reduce_scatter | solution.py:376
  11.5 8.7 %collective-permute-start = (bf16[8,8320]{1,0:T(8,128)(2,1)S(1)}, bf16[8,8320]{1,0:T(8,128)(2,1)S(1)}, u32[]{:S(2)}, u32[]{:S(2)}) collective-permute-start(bf16[8,8320]{1,0:T(8,128)(2,1)S(1)} %pad_maximum_fusion.9), channel_id=1, source_target_pairs={{0,14},{2,0},{4,2},{6,4},{8,6},{10,8},{12,10},{14,12},{1,15},{3,1}... | collective-permute-start | bytes 399368 | tf_op jit(solution)/shard_map/ppermute | solution.py:18
  17.5 6.5 %collective-permute-start.4 = (bf16[8,8320]{1,0:T(8,128)(2,1)S(1)}, bf16[8,8320]{1,0:T(8,128)(2,1)S(1)}, u32[]{:S(2)}, u32[]{:S(2)}) collective-permute-start(bf16[8,8320]{1,0:T(8,128)(2,1)S(1)} %pad_maximum_fusion.9), channel_id=1, source_target_pairs={{0,2},{2,4},{4,6},{6,8},{8,10},{10,12},{12,14},{14,0},{1,3},{3,5},... | collective-permute-start | bytes 399368 | tf_op jit(solution)/shard_map/ppermute | solution.py:18
  20.3 6.2 %collective-permute-start.1 = (bf16[8,8320]{1,0:T(8,128)(2,1)S(1)}, bf16[8,8320]{1,0:T(8,128)(2,1)S(1)}, u32[]{:S(2)}, u32[]{:S(2)}) collective-permute-start(bf16[8,8320]{1,0:T(8,128)(2,1)S(1)} %collective-permute-done), channel_id=1, source_target_pairs={{0,14},{2,0},{4,2},{6,4},{8,6},{10,8},{12,10},{14,12},{1,15},{3,1}... | collective-permute-start | bytes 399368 | tf_op jit(solution)/shard_map/ppermute | solution.py:18
  24.0 6.2 %collective-permute-start.5 = (bf16[8,8320]{1,0:T(8,128)(2,1)S(1)}, bf16[8,8320]{1,0:T(8,128)(2,1)S(1)}, u32[]{:S(2)}, u32[]{:S(2)}) collective-permute-start(bf16[8,8320]{1,0:T(8,128)(2,1)S(1)} %collective-permute-done.4), channel_id=1, source_target_pairs={{0,2},{2,4},{4,6},{6,8},{8,10},{10,12},{12,14},{14,0},{1,3},{3,5},... | collective-permute-start | bytes 399368 | tf_op jit(solution)/shard_map/ppermute | solution.py:18
  26.5 6.2 %collective-permute-start.2 = (bf16[8,8320]{1,0:T(8,128)(2,1)S(1)}, bf16[8,8320]{1,0:T(8,128)(2,1)S(1)}, u32[]{:S(2)}, u32[]{:S(2)}) collective-permute-start(bf16[8,8320]{1,0:T(8,128)(2,1)S(1)} %collective-permute-done.1), channel_id=1, source_target_pairs={{0,14},{2,0},{4,2},{6,4},{8,6},{10,8},{12,10},{14,12},{1,15},{3,1}... | collective-permute-start | bytes 399368 | tf_op jit(solution)/shard_map/ppermute | solution.py:18
  30.2 6.3 %collective-permute-start.6 = (bf16[8,8320]{1,0:T(8,128)(2,1)S(1)}, bf16[8,8320]{1,0:T(8,128)(2,1)S(1)}, u32[]{:S(2)}, u32[]{:S(2)}) collective-permute-start(bf16[8,8320]{1,0:T(8,128)(2,1)S(1)} %collective-permute-done.5), channel_id=1, source_target_pairs={{0,2},{2,4},{4,6},{6,8},{8,10},{10,12},{12,14},{14,0},{1,3},{3,5},... | collective-permute-start | bytes 399368 | tf_op jit(solution)/shard_map/ppermute | solution.py:18
  32.7 9.3 %collective-permute-start.3 = (bf16[8,4224]{1,0:T(8,128)(2,1)S(1)}, bf16[8,4224]{1,0:T(8,128)(2,1)S(1)}, u32[]{:S(2)}, u32[]{:S(2)}) collective-permute-start(bf16[8,4224]{1,0:T(8,128)(2,1)S(1)} %slice.276), channel_id=1, source_target_pairs={{0,14},{2,0},{4,2},{6,4},{8,6},{10,8},{12,10},{14,12},{1,15},{3,1}... | collective-permute-start | bytes 202760 | tf_op jit(solution)/shard_map/ppermute | solution.py:18
  36.4 5.6 %collective-permute-start.9 = (bf16[8,4096]{1,0:T(8,128)(2,1)S(1)}, bf16[8,4096]{1,0:T(8,128)(2,1)S(1)}, u32[]{:S(2)}, u32[]{:S(2)}) collective-permute-start(bf16[8,4096]{1,0:T(8,128)(2,1)S(1)} %slice.283), channel_id=1, source_target_pairs={{0,2},{2,4},{4,6},{6,8},{8,10},{10,12},{12,14},{14,0},{1,3},{3,5},... | collective-permute-start | bytes 196616 | tf_op jit(solution)/shard_map/ppermute | solution.py:18
  42.1 17.2 %collective-permute-start.7 = (bf16[8,8,4224]{2,1,0:T(8,128)(2,1)S(1)}, bf16[8,8,4224]{2,1,0:T(8,128)(2,1)S(1)}, u32[]{:S(2)}, u32[]{:S(2)}) collective-permute-start(bf16[8,8,4224]{2,1,0:T(8,128)(2,1)S(1)} %fusion.25), channel_id=1, source_target_pairs={{0,48},{16,0},{32,16},{48,32},{1,49},{17,1},{33,17},{49,33},{2,50}... | collective-permute-start | bytes 1622024 | tf_op jit(solution)/shard_map/ppermute | solution.py:18
  42.7 16.5 %collective-permute-start.8 = (bf16[8,8,4224]{2,1,0:T(8,128)(2,1)S(1)}, bf16[8,8,4224]{2,1,0:T(8,128)(2,1)S(1)}, u32[]{:S(2)}, u32[]{:S(2)}) collective-permute-start(bf16[8,8,4224]{2,1,0:T(8,128)(2,1)S(1)} %fusion.25), channel_id=1, source_target_pairs={{0,16},{16,32},{32,48},{48,0},{1,17},{17,33},{33,49},{49,1},{2,18}... | collective-permute-start | bytes 1622024 | tf_op jit(solution)/shard_map/ppermute | solution.py:18
  44.2 11.3 %collective-permute-start.10 = (bf16[8,8,4096]{2,1,0:T(8,128)(2,1)S(1)}, bf16[8,8,4096]{2,1,0:T(8,128)(2,1)S(1)}, u32[]{:S(2)}, u32[]{:S(2)}) collective-permute-start(bf16[8,8,4096]{2,1,0:T(8,128)(2,1)S(1)} %fusion.30), channel_id=1, source_target_pairs={{0,192},{64,0},{128,64},{192,128},{1,193},{65,1},{129,65},{193,129... | collective-permute-start | bytes 1572872 | tf_op jit(solution)/shard_map/ppermute | solution.py:18
  47.2 12.0 %collective-permute-start.11 = (bf16[8,8,4096]{2,1,0:T(8,128)(2,1)S(1)}, bf16[8,8,4096]{2,1,0:T(8,128)(2,1)S(1)}, u32[]{:S(2)}, u32[]{:S(2)}) collective-permute-start(bf16[8,8,4096]{2,1,0:T(8,128)(2,1)S(1)} %fusion.30), channel_id=1, source_target_pairs={{0,64},{64,128},{128,192},{192,0},{1,65},{65,129},{129,193},{193,1... | collective-permute-start | bytes 1572872 | tf_op jit(solution)/shard_map/ppermute | solution.py:18
  59.3 6.4 %collective-permute-start.14 = (bf16[4,8,4096]{2,1,0:T(8,128)(2,1)S(1)}, bf16[4,8,4096]{2,1,0:T(8,128)(2,1)S(1)}, u32[]{:S(2)}, u32[]{:S(2)}) collective-permute-start(bf16[4,8,4096]{2,1,0:T(8,128)(2,1)S(1)} %slice.228), channel_id=1, source_target_pairs={{0,192},{64,0},{128,64},{192,128},{1,193},{65,1},{129,65},{193,129... | collective-permute-start | bytes 786440 | tf_op jit(solution)/shard_map/ppermute | solution.py:18
  59.4 7.7 %collective-permute-start.15 = (bf16[4,8,4096]{2,1,0:T(8,128)(2,1)S(1)}, bf16[4,8,4096]{2,1,0:T(8,128)(2,1)S(1)}, u32[]{:S(2)}, u32[]{:S(2)}) collective-permute-start(bf16[4,8,4096]{2,1,0:T(8,128)(2,1)S(1)} %slice.229), channel_id=1, source_target_pairs={{0,64},{64,128},{128,192},{192,0},{1,65},{65,129},{129,193},{193,1... | collective-permute-start | bytes 786440 | tf_op jit(solution)/shard_map/ppermute | solution.py:18
  61.5 7.9 %collective-permute-start.12 = (bf16[4,8,4224]{2,1,0:T(8,128)(2,1)S(1)}, bf16[4,8,4224]{2,1,0:T(8,128)(2,1)S(1)}, u32[]{:S(2)}, u32[]{:S(2)}) collective-permute-start(bf16[4,8,4224]{2,1,0:T(8,128)(2,1)S(1)} %slice.226), channel_id=1, source_target_pairs={{0,48},{16,0},{32,16},{48,32},{1,49},{17,1},{33,17},{49,33},{2,50}... | collective-permute-start | bytes 811016 | tf_op jit(solution)/shard_map/ppermute | solution.py:18
  62.2 9.1 %collective-permute-start.13 = (bf16[4,8,4224]{2,1,0:T(8,128)(2,1)S(1)}, bf16[4,8,4224]{2,1,0:T(8,128)(2,1)S(1)}, u32[]{:S(2)}, u32[]{:S(2)}) collective-permute-start(bf16[4,8,4224]{2,1,0:T(8,128)(2,1)S(1)} %slice.227), channel_id=1, source_target_pairs={{0,16},{16,32},{32,48},{48,0},{1,17},{17,33},{33,49},{49,1},{2,18}... | collective-permute-start | bytes 811016 | tf_op jit(solution)/shard_map/ppermute | solution.py:18
  67.4 13.1 %copy-start.1 = (bf16[4,8,8,4096]{3,2,1,0:T(8,128)(2,1)}, bf16[4,8,8,4096]{3,2,1,0:T(8,128)(2,1)S(1)}, u32[]{:S(2)}) copy-start(bf16[4,8,8,4096]{3,2,1,0:T(8,128)(2,1)S(1)} %pad_maximum_fusion.4.refs_5_.refs_7_) | copy-start | bytes 6291460
  73.8 3.5 copy-start
  74.3 8.0 %collective-permute-start.20 = (bf16[3,192,4096]{2,1,0:T(8,128)(2,1)S(1)}, bf16[3,192,4096]{2,1,0:T(8,128)(2,1)S(1)}, u32[]{:S(2)}, u32[]{:S(2)}) collective-permute-start(bf16[3,192,4096]{2,1,0:T(8,128)(2,1)S(1)} %pad_maximum_fusion.1), channel_id=1, source_target_pairs={{0,1},{1,0},{2,3},{3,2},{4,5},{5,4},{6,7},{7,6},{8,9},{9,8},{10,11... | collective-permute-start | bytes 14155784 | tf_op jit(solution)/shard_map/ppermute | solution.py:18
  74.4 74.8 %collective-permute-start.16 = (bf16[4,8,8,4224]{3,2,1,0:T(8,128)(2,1)S(1)}, bf16[4,8,8,4224]{3,2,1,0:T(8,128)(2,1)S(1)}, u32[]{:S(2)}, u32[]{:S(2)}) collective-permute-start(bf16[4,8,8,4224]{3,2,1,0:T(8,128)(2,1)S(1)} %pad_maximum_fusion.3.refs_0_.refs_2_), channel_id=1, source_target_pairs={{0,192},{64,0},{128,64},{192,128},{1,193},{65,1},{129,65},{193,129... | collective-permute-start | bytes 6488072 | tf_op jit(solution)/shard_map/ppermute | solution.py:18
  77.3 72.8 %collective-permute-start.17 = (bf16[4,8,8,4224]{3,2,1,0:T(8,128)(2,1)S(1)}, bf16[4,8,8,4224]{3,2,1,0:T(8,128)(2,1)S(1)}, u32[]{:S(2)}, u32[]{:S(2)}) collective-permute-start(bf16[4,8,8,4224]{3,2,1,0:T(8,128)(2,1)S(1)} %pad_maximum_fusion.3.refs_0_.refs_2_), channel_id=1, source_target_pairs={{0,64},{64,128},{128,192},{192,0},{1,65},{65,129},{129,193},{193,1... | collective-permute-start | bytes 6488072 | tf_op jit(solution)/shard_map/ppermute | solution.py:18
  77.3 68.0 %collective-permute-start.18 = (bf16[4,8,8,4096]{3,2,1,0:T(8,128)(2,1)S(1)}, bf16[4,8,8,4096]{3,2,1,0:T(8,128)(2,1)S(1)}, u32[]{:S(2)}, u32[]{:S(2)}) collective-permute-start(bf16[4,8,8,4096]{3,2,1,0:T(8,128)(2,1)S(1)} %pad_maximum_fusion.4.refs_5_.refs_7_), channel_id=1, source_target_pairs={{0,48},{16,0},{32,16},{48,32},{1,49},{17,1},{33,17},{49,33},{2,50}... | collective-permute-start | bytes 6291464 | tf_op jit(solution)/shard_map/ppermute | solution.py:18
  80.5 68.2 %collective-permute-start.19 = (bf16[4,8,8,4096]{3,2,1,0:T(8,128)(2,1)S(1)}, bf16[4,8,8,4096]{3,2,1,0:T(8,128)(2,1)S(1)}, u32[]{:S(2)}, u32[]{:S(2)}) collective-permute-start(bf16[4,8,8,4096]{3,2,1,0:T(8,128)(2,1)S(1)} %pad_maximum_fusion.4.refs_5_.refs_7_), channel_id=1, source_target_pairs={{0,16},{16,32},{32,48},{48,0},{1,17},{17,33},{33,49},{49,1},{2,18}... | collective-permute-start | bytes 6291464 | tf_op jit(solution)/shard_map/ppermute | solution.py:18
  145.3 9.9 %copy-start.4 = (bf16[4,8,8,4096]{3,2,1,0:T(8,128)(2,1)}, bf16[4,8,8,4096]{3,2,1,0:T(8,128)(2,1)S(1)}, u32[]{:S(2)}) copy-start(bf16[4,8,8,4096]{3,2,1,0:T(8,128)(2,1)S(1)} %collective-permute-done.18.refs_6_.refs_8_) | copy-start | bytes 6291460
  148.7 10.2 %copy-start.5 = (bf16[4,8,8,4096]{3,2,1,0:T(8,128)(2,1)}, bf16[4,8,8,4096]{3,2,1,0:T(8,128)(2,1)S(1)}, u32[]{:S(2)}) copy-start(bf16[4,8,8,4096]{3,2,1,0:T(8,128)(2,1)S(1)} %collective-permute-done.19.refs_9_.refs_11_) | copy-start | bytes 6291460
  149.3 5.9 %copy-start.2 = (bf16[4,8,8,4224]{3,2,1,0:T(8,128)(2,1)}, bf16[4,8,8,4224]{3,2,1,0:T(8,128)(2,1)S(1)}, u32[]{:S(2)}) copy-start(bf16[4,8,8,4224]{3,2,1,0:T(8,128)(2,1)S(1)} %collective-permute-done.16.refs_1_.refs_3_) | copy-start | bytes 6488068
  150.1 5.1 %copy-start.3 = (bf16[4,8,8,4224]{3,2,1,0:T(8,128)(2,1)}, bf16[4,8,8,4224]{3,2,1,0:T(8,128)(2,1)S(1)}, u32[]{:S(2)}) copy-start(bf16[4,8,8,4224]{3,2,1,0:T(8,128)(2,1)S(1)} %collective-permute-done.17.refs_4_.refs_6_) | copy-start | bytes 6488068
  151.2 46.5 %collective-permute-start.21 = (bf16[2,8,8,4224]{3,2,1,0:T(8,128)(2,1)}, bf16[2,8,8,4224]{3,2,1,0:T(8,128)(2,1)S(1)}, u32[]{:S(2)}, u32[]{:S(2)}) collective-permute-start(bf16[2,8,8,4224]{3,2,1,0:T(8,128)(2,1)} %slice.233), channel_id=1, source_target_pairs={{0,192},{64,0},{128,64},{192,128},{1,193},{65,1},{129,65},{193,129... | collective-permute-start | bytes 3244040 | tf_op jit(solution)/shard_map/ppermute | solution.py:18
  155.2 44.4 %collective-permute-start.22 = (bf16[2,8,8,4224]{3,2,1,0:T(8,128)(2,1)}, bf16[2,8,8,4224]{3,2,1,0:T(8,128)(2,1)S(1)}, u32[]{:S(2)}, u32[]{:S(2)}) collective-permute-start(bf16[2,8,8,4224]{3,2,1,0:T(8,128)(2,1)} %slice.234), channel_id=1, source_target_pairs={{0,64},{64,128},{128,192},{192,0},{1,65},{65,129},{129,193},{193,1... | collective-permute-start | bytes 3244040 | tf_op jit(solution)/shard_map/ppermute | solution.py:18
  156.2 39.3 %collective-permute-start.23 = (bf16[2,8,8,4096]{3,2,1,0:T(8,128)(2,1)}, bf16[2,8,8,4096]{3,2,1,0:T(8,128)(2,1)S(1)}, u32[]{:S(2)}, u32[]{:S(2)}) collective-permute-start(bf16[2,8,8,4096]{3,2,1,0:T(8,128)(2,1)} %slice.235), channel_id=1, source_target_pairs={{0,48},{16,0},{32,16},{48,32},{1,49},{17,1},{33,17},{49,33},{2,50}... | collective-permute-start | bytes 3145736 | tf_op jit(solution)/shard_map/ppermute | solution.py:18
  160.0 36.8 %collective-permute-start.24 = (bf16[2,8,8,4096]{3,2,1,0:T(8,128)(2,1)}, bf16[2,8,8,4096]{3,2,1,0:T(8,128)(2,1)}, u32[]{:S(2)}, u32[]{:S(2)}) collective-permute-start(bf16[2,8,8,4096]{3,2,1,0:T(8,128)(2,1)} %slice.236), channel_id=1, source_target_pairs={{0,16},{16,32},{32,48},{48,0},{1,17},{17,33},{33,49},{49,1},{2,18}... | collective-permute-start | bytes 3145736 | tf_op jit(solution)/shard_map/ppermute | solution.py:18
  195.5 4.0 copy-start.12
  236.4 39.2 %collective-permute-start.27 = (bf16[2,8,8,4096]{3,2,1,0:T(8,128)(2,1)}, bf16[2,8,8,4096]{3,2,1,0:T(8,128)(2,1)S(1)}, u32[]{:S(2)}, u32[]{:S(2)}) collective-permute-start(bf16[2,8,8,4096]{3,2,1,0:T(8,128)(2,1)} %get-tuple-element.121), channel_id=1, source_target_pairs={{0,16},{16,32},{32,48},{48,0},{1,17},{17,33},{33,49},{49,1},{2,18}... | collective-permute-start | bytes 3145736 | tf_op jit(solution)/shard_map/ppermute | solution.py:18
  237.6 38.0 %collective-permute-start.28 = (bf16[2,8,8,4096]{3,2,1,0:T(8,128)(2,1)}, bf16[2,8,8,4096]{3,2,1,0:T(8,128)(2,1)}, u32[]{:S(2)}, u32[]{:S(2)}) collective-permute-start(bf16[2,8,8,4096]{3,2,1,0:T(8,128)(2,1)} %get-tuple-element.120), channel_id=1, source_target_pairs={{0,48},{16,0},{32,16},{48,32},{1,49},{17,1},{33,17},{49,33},{2,50}... | collective-permute-start | bytes 3145736 | tf_op jit(solution)/shard_map/ppermute | solution.py:18
  252.9 25.7 %collective-permute-start.25 = (bf16[2,8,8,4096]{3,2,1,0:T(8,128)(2,1)S(1)}, bf16[2,8,8,4096]{3,2,1,0:T(8,128)(2,1)S(1)}, u32[]{:S(2)}, u32[]{:S(2)}) collective-permute-start(bf16[2,8,8,4096]{3,2,1,0:T(8,128)(2,1)S(1)} %get-tuple-element.143), channel_id=1, source_target_pairs={{0,64},{64,128},{128,192},{192,0},{1,65},{65,129},{129,193},{193,1... | collective-permute-start | bytes 3145736 | tf_op jit(solution)/shard_map/ppermute | solution.py:18
  253.8 24.8 %collective-permute-start.26 = (bf16[2,8,8,4096]{3,2,1,0:T(8,128)(2,1)S(1)}, bf16[2,8,8,4096]{3,2,1,0:T(8,128)(2,1)S(1)}, u32[]{:S(2)}, u32[]{:S(2)}) collective-permute-start(bf16[2,8,8,4096]{3,2,1,0:T(8,128)(2,1)S(1)} %get-tuple-element.142), channel_id=1, source_target_pairs={{0,192},{64,0},{128,64},{192,128},{1,193},{65,1},{129,65},{193,129... | collective-permute-start | bytes 3145736 | tf_op jit(solution)/shard_map/ppermute | solution.py:18
  283.6 52.4 %collective-permute-start.30 = (bf16[4,8,8,4096]{3,2,1,0:T(8,128)(2,1)}, bf16[4,8,8,4096]{3,2,1,0:T(8,128)(2,1)}, u32[]{:S(2)}, u32[]{:S(2)}) collective-permute-start(bf16[4,8,8,4096]{3,2,1,0:T(8,128)(2,1)} %pad_maximum_fusion.6), channel_id=1, source_target_pairs={{0,192},{64,0},{128,64},{192,128},{1,193},{65,1},{129,65},{193,129... | collective-permute-start | bytes 6291464 | tf_op jit(solution)/shard_map/ppermute | solution.py:18
  288.2 47.8 %collective-permute-start.29 = (bf16[4,8,8,4096]{3,2,1,0:T(8,128)(2,1)}, bf16[4,8,8,4096]{3,2,1,0:T(8,128)(2,1)}, u32[]{:S(2)}, u32[]{:S(2)}) collective-permute-start(bf16[4,8,8,4096]{3,2,1,0:T(8,128)(2,1)} %pad_maximum_fusion.5), channel_id=1, source_target_pairs={{0,64},{64,128},{128,192},{192,0},{1,65},{65,129},{129,193},{193,1... | collective-permute-start | bytes 6291464 | tf_op jit(solution)/shard_map/ppermute | solution.py:18
  292.4 46.0 %collective-permute-start.36 = (bf16[4,8,8,4096]{3,2,1,0:T(8,128)(2,1)}, bf16[4,8,8,4096]{3,2,1,0:T(8,128)(2,1)}, u32[]{:S(2)}, u32[]{:S(2)}) collective-permute-start(bf16[4,8,8,4096]{3,2,1,0:T(8,128)(2,1)} %pad_maximum_fusion.8), channel_id=1, source_target_pairs={{0,48},{16,0},{32,16},{48,32},{1,49},{17,1},{33,17},{49,33},{2,50}... | collective-permute-start | bytes 6291464 | tf_op jit(solution)/shard_map/ppermute | solution.py:18
  295.6 45.4 %collective-permute-start.35 = (bf16[4,8,8,4096]{3,2,1,0:T(8,128)(2,1)S(1)}, bf16[4,8,8,4096]{3,2,1,0:T(8,128)(2,1)}, u32[]{:S(2)}, u32[]{:S(2)}) collective-permute-start(bf16[4,8,8,4096]{3,2,1,0:T(8,128)(2,1)S(1)} %pad_maximum_fusion.7), channel_id=1, source_target_pairs={{0,16},{16,32},{32,48},{48,0},{1,17},{17,33},{33,49},{49,1},{2,18}... | collective-permute-start | bytes 6291464 | tf_op jit(solution)/shard_map/ppermute | solution.py:18
  340.9 38.8 %collective-permute-start.37 = (bf16[3,192,4096]{2,1,0:T(8,128)(2,1)}, bf16[3,192,4096]{2,1,0:T(8,128)(2,1)}, u32[]{:S(2)}, u32[]{:S(2)}) collective-permute-start(bf16[3,192,4096]{2,1,0:T(8,128)(2,1)} %get-tuple-element.106), channel_id=1, source_target_pairs={{0,1},{1,0},{2,3},{3,2},{4,5},{5,4},{6,7},{7,6},{8,9},{9,8},{10,11... | collective-permute-start | bytes 14155784 | tf_op jit(solution)/shard_map/ppermute | solution.py:18
  340.9 11.2 %copy-start.15 = (bf16[1,4,8,8,4096]{4,3,2,1,0:T(8,128)(2,1)S(1)}, bf16[1,4,8,8,4096]{4,3,2,1,0:T(8,128)(2,1)}, u32[]{:S(2)}) copy-start(bf16[1,4,8,8,4096]{4,3,2,1,0:T(8,128)(2,1)} %get-tuple-element.87) | copy-start | bytes 6291460
  340.9 38.8 %slice-start = ((s8[9437184]{0:T(1024)(128)(4,1)}), s8[4194304]{0:T(1024)(128)(4,1)S(1)}, s32[]{:S(2)}) async-start(s8[9437184]{0:T(1024)(128)(4,1)} %bitcast.165), calls=%async_computation.3 | async-start | bytes 8388608
  345.0 34.7 %slice-start.1 = ((s8[9437184]{0:T(1024)(128)(4,1)}), s8[4194304]{0:T(1024)(128)(4,1)S(1)}, s32[]{:S(2)}) async-start(s8[9437184]{0:T(1024)(128)(4,1)} %bitcast.165), calls=%async_computation.4 | async-start | bytes 8388608
  345.1 30.0 %collective-permute-start.45 = (bf16[8,8,4096]{2,1,0:T(8,128)(2,1)S(1)}, bf16[8,8,4096]{2,1,0:T(8,128)(2,1)S(1)}, u32[]{:S(2)}, u32[]{:S(2)}) collective-permute-start(bf16[8,8,4096]{2,1,0:T(8,128)(2,1)S(1)} %get-tuple-element.141), channel_id=1, source_target_pairs={{0,64},{64,128},{128,192},{192,0},{1,65},{65,129},{129,193},{193,1... | collective-permute-start | bytes 1572872 | tf_op jit(solution)/shard_map/ppermute | solution.py:18
  345.2 29.9 %collective-permute-start.46 = (bf16[8,8,4096]{2,1,0:T(8,128)(2,1)S(1)}, bf16[8,8,4096]{2,1,0:T(8,128)(2,1)S(1)}, u32[]{:S(2)}, u32[]{:S(2)}) collective-permute-start(bf16[8,8,4096]{2,1,0:T(8,128)(2,1)S(1)} %get-tuple-element.140), channel_id=1, source_target_pairs={{0,192},{64,0},{128,64},{192,128},{1,193},{65,1},{129,65},{193,129... | collective-permute-start | bytes 1572872 | tf_op jit(solution)/shard_map/ppermute | solution.py:18
  348.5 19.5 %collective-permute-start.47 = (bf16[4,8,4096]{2,1,0:T(8,128)(2,1)S(1)}, bf16[4,8,4096]{2,1,0:T(8,128)(2,1)S(1)}, u32[]{:S(2)}, u32[]{:S(2)}) collective-permute-start(bf16[4,8,4096]{2,1,0:T(8,128)(2,1)S(1)} %get-tuple-element.139), channel_id=1, source_target_pairs={{0,128},{64,192},{128,0},{192,64},{1,129},{65,193},{129,1},{193,65... | collective-permute-start | bytes 786440 | tf_op jit(solution)/shard_map/ppermute | solution.py:18
  349.7 23.4 %collective-permute-start.48 = (bf16[4,8,4096]{2,1,0:T(8,128)(2,1)S(1)}, bf16[4,8,4096]{2,1,0:T(8,128)(2,1)S(1)}, u32[]{:S(2)}, u32[]{:S(2)}) collective-permute-start(bf16[4,8,4096]{2,1,0:T(8,128)(2,1)S(1)} %get-tuple-element.138), channel_id=1, source_target_pairs={{0,128},{64,192},{128,0},{192,64},{1,129},{65,193},{129,1},{193,65... | collective-permute-start | bytes 786440 | tf_op jit(solution)/shard_map/ppermute | solution.py:18
  352.1 27.7 %slice-start.2 = ((s8[9437184]{0:T(1024)(128)(4,1)}), s8[1048576]{0:T(1024)(128)(4,1)S(1)}, s32[]{:S(2)}) async-start(s8[9437184]{0:T(1024)(128)(4,1)} %bitcast.165), calls=%async_computation.5 | async-start | bytes 2097152
  355.4 24.3 %copy-start.6 = (bf16[4,8,8,4096]{3,2,1,0:T(8,128)(2,1)}, bf16[4,8,8,4096]{3,2,1,0:T(8,128)(2,1)S(1)}, u32[]{:S(2)}) copy-start(bf16[4,8,8,4096]{3,2,1,0:T(8,128)(2,1)S(1)} %fusion.3) | copy-start | bytes 6291460
  367.9 30.4 %collective-permute-start.31 = (bf16[8,8,4096]{2,1,0:T(8,128)(2,1)}, bf16[8,8,4096]{2,1,0:T(8,128)(2,1)}, u32[]{:S(2)}, u32[]{:S(2)}) collective-permute-start(bf16[8,8,4096]{2,1,0:T(8,128)(2,1)} %get-tuple-element.137), channel_id=1, source_target_pairs={{0,16},{16,32},{32,48},{48,0},{1,17},{17,33},{33,49},{49,1},{2,18}... | collective-permute-start | bytes 1572872 | tf_op jit(solution)/shard_map/ppermute | solution.py:18
  373.2 25.3 %collective-permute-start.32 = (bf16[8,8,4096]{2,1,0:T(8,128)(2,1)}, bf16[8,8,4096]{2,1,0:T(8,128)(2,1)}, u32[]{:S(2)}, u32[]{:S(2)}) collective-permute-start(bf16[8,8,4096]{2,1,0:T(8,128)(2,1)} %get-tuple-element.136), channel_id=1, source_target_pairs={{0,48},{16,0},{32,16},{48,32},{1,49},{17,1},{33,17},{49,33},{2,50}... | collective-permute-start | bytes 1572872 | tf_op jit(solution)/shard_map/ppermute | solution.py:18
  375.1 18.8 %collective-permute-start.33 = (bf16[4,8,4096]{2,1,0:T(8,128)(2,1)}, bf16[4,8,4096]{2,1,0:T(8,128)(2,1)}, u32[]{:S(2)}, u32[]{:S(2)}) collective-permute-start(bf16[4,8,4096]{2,1,0:T(8,128)(2,1)} %get-tuple-element.135), channel_id=1, source_target_pairs={{0,32},{16,48},{32,0},{48,16},{1,33},{17,49},{33,1},{49,17},{2,34}... | collective-permute-start | bytes 786440 | tf_op jit(solution)/shard_map/ppermute | solution.py:18
  375.1 23.2 %collective-permute-start.34 = (bf16[4,8,4096]{2,1,0:T(8,128)(2,1)S(1)}, bf16[4,8,4096]{2,1,0:T(8,128)(2,1)}, u32[]{:S(2)}, u32[]{:S(2)}) collective-permute-start(bf16[4,8,4096]{2,1,0:T(8,128)(2,1)S(1)} %get-tuple-element.134), channel_id=1, source_target_pairs={{0,32},{16,48},{32,0},{48,16},{1,33},{17,49},{33,1},{49,17},{2,34}... | collective-permute-start | bytes 786440 | tf_op jit(solution)/shard_map/ppermute | solution.py:18
  386.1 15.0 %copy-start.14 = (bf16[8,8,4096]{2,1,0:T(8,128)(2,1)S(1)}, bf16[8,8,4096]{2,1,0:T(8,128)(2,1)}, u32[]{:S(2)}) copy-start(bf16[8,8,4096]{2,1,0:T(8,128)(2,1)} %fusion.10) | copy-start | bytes 1572868
  400.3 11.1 %collective-permute-start.38 = (bf16[8,4096]{1,0:T(8,128)(2,1)S(1)}, bf16[8,4096]{1,0:T(8,128)(2,1)S(1)}, u32[]{:S(2)}, u32[]{:S(2)}) collective-permute-start(bf16[8,4096]{1,0:T(8,128)(2,1)S(1)} %get-tuple-element.144), channel_id=1, source_target_pairs={{0,2},{2,4},{4,6},{6,8},{8,10},{10,12},{12,14},{14,0},{1,3},{3,5},... | collective-permute-start | bytes 196616 | tf_op jit(solution)/shard_map/ppermute | solution.py:18
  401.1 11.6 %collective-permute-start.39 = (bf16[8,4096]{1,0:T(8,128)(2,1)S(1)}, bf16[8,4096]{1,0:T(8,128)(2,1)S(1)}, u32[]{:S(2)}, u32[]{:S(2)}) collective-permute-start(bf16[8,4096]{1,0:T(8,128)(2,1)S(1)} %get-tuple-element.150), channel_id=1, source_target_pairs={{0,4},{2,6},{4,8},{6,10},{8,12},{10,14},{12,0},{14,2},{1,5},{3,7},... | collective-permute-start | bytes 196616 | tf_op jit(solution)/shard_map/ppermute | solution.py:18
  402.2 19.4 %collective-permute-start.40 = (bf16[8,4096]{1,0:T(8,128)(2,1)S(1)}, bf16[8,4096]{1,0:T(8,128)(2,1)S(1)}, u32[]{:S(2)}, u32[]{:S(2)}) collective-permute-start(bf16[8,4096]{1,0:T(8,128)(2,1)S(1)} %get-tuple-element.149), channel_id=1, source_target_pairs={{0,6},{2,8},{4,10},{6,12},{8,14},{10,0},{12,2},{14,4},{1,7},{3,9},... | collective-permute-start | bytes 196616 | tf_op jit(solution)/shard_map/ppermute | solution.py:18
  406.2 15.3 %collective-permute-start.41 = (bf16[8,4096]{1,0:T(8,128)(2,1)S(1)}, bf16[8,4096]{1,0:T(8,128)(2,1)S(1)}, u32[]{:S(2)}, u32[]{:S(2)}) collective-permute-start(bf16[8,4096]{1,0:T(8,128)(2,1)S(1)} %get-tuple-element.148), channel_id=1, source_target_pairs={{0,10},{2,12},{4,14},{6,0},{8,2},{10,4},{12,6},{14,8},{1,11},{3,13... | collective-permute-start | bytes 196616 | tf_op jit(solution)/shard_map/ppermute | solution.py:18
  407.3 14.3 %collective-permute-start.42 = (bf16[8,4096]{1,0:T(8,128)(2,1)S(1)}, bf16[8,4096]{1,0:T(8,128)(2,1)S(1)}, u32[]{:S(2)}, u32[]{:S(2)}) collective-permute-start(bf16[8,4096]{1,0:T(8,128)(2,1)S(1)} %get-tuple-element.147), channel_id=1, source_target_pairs={{0,12},{2,14},{4,0},{6,2},{8,4},{10,6},{12,8},{14,10},{1,13},{3,15... | collective-permute-start | bytes 196616 | tf_op jit(solution)/shard_map/ppermute | solution.py:18
  411.4 10.2 %collective-permute-start.43 = (bf16[8,4096]{1,0:T(8,128)(2,1)S(1)}, bf16[8,4096]{1,0:T(8,128)(2,1)S(1)}, u32[]{:S(2)}, u32[]{:S(2)}) collective-permute-start(bf16[8,4096]{1,0:T(8,128)(2,1)S(1)} %get-tuple-element.146), channel_id=1, source_target_pairs={{0,14},{2,0},{4,2},{6,4},{8,6},{10,8},{12,10},{14,12},{1,15},{3,1}... | collective-permute-start | bytes 196616 | tf_op jit(solution)/shard_map/ppermute | solution.py:18
  412.7 8.9 %collective-permute-start.44 = (bf16[8,4096]{1,0:T(8,128)(2,1)S(1)}, bf16[8,4096]{1,0:T(8,128)(2,1)S(1)}, u32[]{:S(2)}, u32[]{:S(2)}) collective-permute-start(bf16[8,4096]{1,0:T(8,128)(2,1)S(1)} %get-tuple-element.145), channel_id=1, source_target_pairs={{0,8},{2,10},{4,12},{6,14},{8,0},{10,2},{12,4},{14,6},{1,9},{3,11}... | collective-permute-start | bytes 196616 | tf_op jit(solution)/shard_map/ppermute | solution.py:18
  (6 other events, 11.4 us)
Sparse Core Ops, SparseCore 0:
  11.9 198.4 all-gather.1
  402.3 37.2 reduce-scatter.1
